TPU v7x, 512 devices: a whole 4x8x8 slice. The times are simulated.
512 devices in a mesh: left: 16 (over x, y_hi, core), right: 32 (over y_lo, z).
Axes of the slice: x: 4, y: 8 (y_hi: 2, y_lo: 4; y = y_hi * 4 + y_lo), z: 8, core: 2. Of those that a mesh axis runs over, the one named last changes fastest.
Arguments:
- left_table: bfloat16 [32768, 256], P('left'), may hold values from -1.5 to 1.5
- right_table: bfloat16 [16, 16384, 256], P('left', 'right'), may hold values from -1.5 to 1.5
- relations: float32 [512, 256], replicated, may hold values from -6 to 6
- source_ids: int32 [16, 32, 1024], P('left', 'right'), may hold values from 0 to 2047
- relation_ids: int32 [16, 32, 1024], P('left', 'right'), may hold values from 0 to 511
- target_ids: int32 [16, 32, 1024], P('left', 'right'), may hold values from 0 to 511
- negative_ids: int32 [16, 32, 1, 1024], P('left', 'right'), may hold values from 0 to 511
- edge_counts: int32 [16, 32], P('left', 'right'), may hold values from 1 to 1024
Outputs:
- left_next: bfloat16 [32768, 256], P('left')
- right_next: bfloat16 [16, 16384, 256], P('left', 'right')
- relations_next: float32 [512, 256], replicated
Inputs may be any that keep to these rules, and one draw needn't show every extreme that they name: Edge slots at positions from edge_counts to 1023 hold ids but are padding.
All inputs are finite; a program needn't handle non-finite values.
Results may differ from a plain program's by a relative error of at most 0.0013.
Values may be sent and summed in bfloat16 or wider, within the bound.
No kernel may reach another device: no remote copies, remote signals or barrier semaphores. Data moves between devices by JAX's collectives and lax.ppermute only.
A program may use at most 64 MiB of HBM per device.

v0:
```python
import jax
import jax.numpy as jnp
from jax import lax
from jax.sharding import PartitionSpec as P

step_size = 0.5
relation_step = 12.0


def passed_along(array, axis, by):
    peers = lax.axis_size(axis)
    return lax.ppermute(array, axis, [(i, (i + by) % peers) for i in range(peers)])


def block_terms(left_blk, right_blk, relations, src, kind, dst, neg, live):
    half = relations.shape[1] // 2
    head = jnp.take(left_blk, src, axis=0).astype(jnp.float32)
    tail = jnp.take(right_blk, dst, axis=0).astype(jnp.float32)
    rel = jnp.take(relations, kind, axis=0)
    hre, him = (head[:, :half], head[:, half:])
    rre, rim = (rel[:, :half], rel[:, half:])
    query = jnp.concatenate([hre * rre - him * rim, hre * rim + him * rre], axis=1)
    q_low = query.astype(jnp.bfloat16)
    pos = jnp.sum(query * tail, axis=1)
    negrows = jnp.take(right_blk, neg, axis=0)
    scores = lax.dot_general(
        q_low, negrows, (((1,), (1,)), ((), ())), preferred_element_type=jnp.float32
    )
    c_pos = -jax.nn.sigmoid(-pos) * live
    c_neg = (jax.nn.sigmoid(scores) * (live[:, None] / neg.shape[0])).astype(jnp.bfloat16)
    g_query = jnp.dot(c_neg, negrows, preferred_element_type=jnp.float32) + c_pos[:, None] * tail
    g_neg = lax.dot_general(
        c_neg, q_low, (((0,), (0,)), ((), ())), preferred_element_type=jnp.float32
    )
    g_tail = c_pos[:, None] * query
    gre, gim = (g_query[:, :half], g_query[:, half:])
    grad_h = jnp.concatenate([gre * rre + gim * rim, -gre * rim + gim * rre], axis=1)
    grad_r = jnp.concatenate([gre * hre + gim * him, -gre * him + gim * hre], axis=1)
    return (grad_h, grad_r, g_tail, g_neg)


def shards(
    left_table,
    right_table,
    relations,
    source_ids,
    relation_ids,
    target_ids,
    negative_ids,
    edge_counts,
):
    right_blk = right_table[0]
    src_all = source_ids[0, 0]
    kind_all = relation_ids[0, 0]
    dst_all = target_ids[0, 0]
    negs = negative_ids[0, 0]
    count = edge_counts[0, 0]
    blocks = negs.shape[0]
    width = src_all.shape[0] // blocks
    live_blocks = (count + width - 1) // width

    def one(index, carry):
        lgrad, rgrad, tgrad = carry
        start = index * width
        n = lax.dynamic_index_in_dim(negs, index, 0, keepdims=False)
        live = (start + jnp.arange(width, dtype=jnp.int32) < count).astype(jnp.float32)
        grad_h, grad_r, g_tail, g_neg = block_terms(
            left_table, right_blk, relations, src_all, kind_all, dst_all, n, live
        )
        lgrad = lgrad.at[src_all].add(grad_h)
        rgrad = rgrad.at[kind_all].add(grad_r)
        tgrad = tgrad.at[dst_all].add(g_tail).at[n].add(g_neg)
        return (lgrad, rgrad, tgrad)

    init = (
        jnp.zeros(left_table.shape, jnp.float32),
        jnp.zeros(relations.shape, jnp.float32),
        jnp.zeros(right_blk.shape, jnp.float32),
    )
    left_grad, rel_grad, right_grad = lax.fori_loop(0, live_blocks, one, init)
    updated = (right_blk.astype(jnp.float32) - step_size * right_grad).astype(jnp.bfloat16)
    moved = passed_along(updated, "right", 1)
    left_total = lax.psum(left_grad, "right")
    rel_total = lax.psum(rel_grad, ("left", "right"))
    left_next = (left_table.astype(jnp.float32) - step_size * left_total).astype(jnp.bfloat16)
    relations_next = relations - relation_step * rel_total
    return (left_next, moved[None], relations_next)


def solution(mesh):
    return jax.shard_map(
        shards,
        mesh=mesh,
        in_specs=(
            P("left", None),
            P("left", "right", None),
            P(),
            P("left", "right", None),
            P("left", "right", None),
            P("left", "right", None),
            P("left", "right", None, None),
            P("left", "right"),
        ),
        out_specs=(P("left", None), P("left", "right", None), P()),
        check_vma=False,
    )
```

profile of v0, /device:TPU:2, one launch (start us, length us, event | category | flops | bytes accessed | tf_op | source)
XLA Modules:
  0.0 709.8 jit_solution(15141002125790694229)
XLA Ops:
  12.0 4.9 gather_fusion.4
  16.9 3.9 gather_fusion.6
  21.1 3.5 gather_fusion.5
  25.5 1.4 broadcast_in_dim.66
  26.9 80.2 %while.17 = (s32[]{:T(128)}, f32[2048,256]{1,0:T(8,128)}, f32[512,256]{1,0:T(8,128)S(1)}, f32[512,256]{1,0:T(8,128)S(1)}, s32[]{:T(128)}, /*index=5*/s32[1024]{0...) while((s32[]{:T(128)}, f32[2048,256]{1,0:T(8,128)}, ...), condition=%wide.region_6.8_spmd, body=%wide.region_1.7_spmd.sunk | while | flops 1624953856 | bytes 75646288 | solution.py:80
  28.0 5.0 gather_fusion
  32.9 3.9 gather_fusion.3
  37.9 5.0 gather_fusion.2
  42.9 1.2 copy.27
  44.1 1.0 select_convert_fusion.3
  45.2 4.7 gather_fusion.1
  49.8 2.6 copy.26
  52.4 1.4 broadcast_select_fusion.10
  55.8 1.1 fusion.30
  56.9 2.5 copy.31
  59.4 6.7 scatter_fusion.2
  66.2 3.0 multiply_convert_fusion.2
  69.2 1.8 convolution_add_fusion.2
  71.0 1.8 fusion.31
  72.8 6.7 scatter_fusion.3
  79.5 3.0 multiply_add_fusion.7
  82.6 1.0 pad_maximum_fusion.5
  83.6 2.5 copy.29
  86.1 9.4 %scatter_fusion = f32[2048,256]{1,0:T(8,128)} fusion(f32[2048,256]{1,0:T(8,128)} %get-tuple-element.393, s32[1024]{0:T(1024)S(1)} %bitcast.59, f32[1024,256]{1,0:T(8,128)} %copy.29), kind=kCustom, calls=%fused_computation.7.clone.1 | custom fusion | flops 262144 | bytes 3149824 | tf_op jit(solution)/shard_map/while/body/scatter-add | solution.py:70
  95.5 2.1 pad_maximum_fusion.6
  97.6 2.5 copy.30
  100.1 6.7 scatter_fusion.1
  108.8 4.3 collective-permute-start
  113.0 270.8 %all-reduce.5.cloned.1.call-done = f32[512,256]{1,0:T(8,128)} async-done(((f32[512,256]{1,0:T(8,128)}), f32[512,256]{1,0:T(8,128)}) %all-reduce.5.cloned.1.call-update) | async-done | bytes 524304 | tf_op jit(solution)/shard_map/psum | solution.py:84
  383.8 1.9 multiply_subtract_fusion.1
  385.7 313.7 %all-reduce.3.cloned.1.call-done = f32[2048,256]{1,0:T(8,128)} async-done(((f32[2048,256]{1,0:T(8,128)}), f32[2048,256]{1,0:T(8,128)}) %all-reduce.3.cloned.1.call-update) | async-done | bytes 2097168 | tf_op jit(solution)/shard_map/psum | solution.py:83
  699.4 2.8 subtract_convert_fusion
  (64 shorter events, 11.2 us)
Async XLA Ops:
  7.2 376.7 %all-reduce.5.cloned.1.call-start = ((), (), s32[]{:S(2)}) async-start(), calls=%async_computation.1 | async-start | bytes 1048576 | tf_op jit(solution)/shard_map/psum | solution.py:84
  12.0 4.9 copy-start
  16.9 4.2 copy-start.1
  24.9 2.0 copy-start.3
  24.9 2.0 copy-start.10
  24.9 2.0 copy-start.11
  25.0 2.0 copy-start.12
  25.0 2.0 copy-start.13
  52.4 1.5 copy-start.4
  54.0 1.0 copy-start.5
  55.0 0.8 copy-start.6
  66.2 3.0 copy-start.8
  66.2 3.0 copy-start.9
  69.2 1.8 copy-start.7
  107.1 0.8 copy-start.2
  107.9 591.5 %all-reduce.3.cloned.1.call-start = ((), (), s32[]{:S(2)}) async-start(), calls=%async_computation | async-start | bytes 4194304 | tf_op jit(solution)/shard_map/psum | solution.py:83
  108.8 277.0 %collective-permute-start = (bf16[512,256]{1,0:T(8,128)(2,1)S(1)}, bf16[512,256]{1,0:T(8,128)(2,1)S(1)}, u32[]{:S(2)}, u32[]{:S(2)}) collective-permute-start(bf16[512,256]{1,0:T(8,128)(2,1)S(1)} %subtract_convert_fusion.1), channel_id=1, source_target_pairs={{0,1},{1,2},{2,3},{3,4},{4,5},{5,6},{6,7},{7,8},{8,9},{9,10},{10,1... | collective-permute-start | bytes 786440 | tf_op jit(solution)/shard_map/ppermute | solution.py:12
Sparse Core Ops, SparseCore 0:
  108.1 275.7 all-reduce.4
  386.7 312.6 all-reduce.2
where the time goes:
time: 711 us; the launch traced here: 710 us
  waiting for transfers between devices  585 us (82%)
  other arithmetic  50.1 us (7%)
  local copies, waits for them, and re-layouts  48.1 us (7%)
  between operations  14.9 us (2%)
    psum x1, waiting for transfers between devices, shards(): left_total = lax.psum(left_grad, 'right')  314 us
    psum x1, waiting for transfers between devices, shards(): rel_total = lax.psum(rel_grad, ('left', 'right'))  271 us
  transfers between devices with their start and end apart: 3, of which 2 were waited for; matrix products, arithmetic and copies ran while one was open for 0% of the time, Pallas kernels for 0%

commit v1 on v0

v1 whole, which is shorter than its diff:
```python
import functools

import jax
import jax.numpy as jnp
from jax import lax
from jax.experimental import pallas as pl
from jax.experimental.pallas import tpu as pltpu
from jax.sharding import PartitionSpec as P

step_size = 0.5
relation_step = 12.0
EDGES = 256
ROWS = 256
F32 = jnp.float32
BF16 = jnp.bfloat16


def passed_along(array, axis, by):
    peers = lax.axis_size(axis)
    return lax.ppermute(array, axis, [(i, (i + by) % peers) for i in range(peers)])


def mm(a, b):
    return lax.dot_general(a, b, (((1,), (0,)), ((), ())), preferred_element_type=F32)


def mm_nt(a, b):
    return lax.dot_general(a, b, (((1,), (1,)), ((), ())), preferred_element_type=F32)


def two_parts(x):
    high = x.astype(BF16)
    return high, (x - high.astype(F32)).astype(BF16)


def one_hot(rows, ids):
    return jnp.where(lax.broadcasted_iota(jnp.int32, (rows, ids.shape[1]), 0) == ids, 1.0, 0.0)


def bucket_kernel(
    count_ref, src_ref, kind_ref, dst_ref, neg_ref, left_ref, right_ref, rel_ref,
    lgrad_ref, rgrad_ref, right_new_ref,
    oh_src, gh_high, gh_low, left_t, right_t, rel_high_t, rel_low_t, tgrad,
):
    n_left, width = left_ref.shape
    n_right, n_rel = right_ref.shape[0], rel_ref.shape[0]
    half = width // 2
    blocks = src_ref.shape[0]
    negs = neg_ref.shape[0] * neg_ref.shape[2]
    count = count_ref[0]
    eye = jnp.where(
        lax.broadcasted_iota(jnp.int32, (width, width), 0)
        == lax.broadcasted_iota(jnp.int32, (width, width), 1),
        1.0,
        0.0,
    ).astype(BF16)
    left_t[...] = mm_nt(eye, left_ref[...]).astype(BF16)
    right_t[...] = mm_nt(eye, right_ref[...]).astype(BF16)
    rel_high, rel_low = two_parts(rel_ref[...])
    rel_high_t[...] = mm_nt(eye, rel_high).astype(BF16)
    rel_low_t[...] = mm_nt(eye, rel_low).astype(BF16)
    seen = one_hot(n_right, neg_ref[0])
    for i in range(1, neg_ref.shape[0]):
        seen = seen + one_hot(n_right, neg_ref[i])
    times = jnp.sum(seen, axis=1, keepdims=True) * (1.0 / negs)
    rgrad_ref[...] = jnp.zeros_like(rgrad_ref)
    tgrad[...] = jnp.zeros_like(tgrad)

    def block(i, carry):
        ohs = one_hot(n_left, src_ref[i]).astype(BF16)
        ohk = one_hot(n_rel, kind_ref[i]).astype(BF16)
        ohd = one_hot(n_right, dst_ref[i]).astype(BF16)
        oh_src[i] = ohs
        head = mm(left_t[...], ohs)
        tail = mm(right_t[...], ohd)
        rel = mm(rel_high_t[...], ohk) + mm(rel_low_t[...], ohk)
        hre, him = head[:half], head[half:]
        rre, rim = rel[:half], rel[half:]
        query = jnp.concatenate([hre * rre - him * rim, hre * rim + him * rre], axis=0)
        q_low = query.astype(BF16)
        pos = jnp.sum(query * tail, axis=0, keepdims=True)
        slot = i * EDGES + lax.broadcasted_iota(jnp.int32, (1, EDGES), 1)
        live = jnp.where(slot < count, 1.0, 0.0)
        c_pos = -jax.nn.sigmoid(-pos) * live
        scores = mm(right_ref[...], q_low)
        c_neg = (jax.nn.sigmoid(scores) * (times * live)).astype(BF16)
        g_query = mm(right_t[...], c_neg) + c_pos * tail
        gre, gim = g_query[:half], g_query[half:]
        grad_h = jnp.concatenate([gre * rre + gim * rim, -gre * rim + gim * rre], axis=0)
        grad_r = jnp.concatenate([gre * hre + gim * him, -gre * him + gim * hre], axis=0)
        gh_high[i], gh_low[i] = two_parts(grad_h)
        rgrad_ref[...] += mm_nt(ohk, grad_r.astype(BF16))
        t_high, t_low = two_parts(c_pos * query)
        tgrad[...] += mm_nt(c_neg, q_low) + mm_nt(ohd, t_high) + mm_nt(ohd, t_low)
        return carry

    lax.fori_loop(0, blocks, block, 0)
    right_new_ref[...] = (right_ref[...].astype(F32) - step_size * tgrad[...]).astype(BF16)

    def rows(j, carry):
        at = pl.ds(pl.multiple_of(j * ROWS, ROWS), ROWS)
        total = jnp.zeros((ROWS, width), F32)
        for i in range(blocks):
            hot = oh_src[i, at, :]
            total += mm_nt(hot, gh_high[i]) + mm_nt(hot, gh_low[i])
        lgrad_ref[at, :] = total
        return carry

    lax.fori_loop(0, n_left // ROWS, rows, 0)


def bucket_grads(count, src, kind, dst, neg, left_blk, right_blk, relations, interpret=False):
    n_left, width = left_blk.shape
    n_right, n_rel, edges = right_blk.shape[0], relations.shape[0], src.size
    blocks = edges // EDGES
    vmem = pl.BlockSpec(memory_space=pltpu.VMEM)
    return pl.pallas_call(
        bucket_kernel,
        out_shape=(
            jax.ShapeDtypeStruct((n_left, width), F32),
            jax.ShapeDtypeStruct((n_rel, width), F32),
            jax.ShapeDtypeStruct((n_right, width), BF16),
        ),
        in_specs=[pl.BlockSpec(memory_space=pltpu.SMEM)] + [vmem] * 7,
        out_specs=(vmem, vmem, vmem),
        scratch_shapes=[
            pltpu.VMEM((blocks, n_left, EDGES), BF16),
            pltpu.VMEM((blocks, width, EDGES), BF16),
            pltpu.VMEM((blocks, width, EDGES), BF16),
            pltpu.VMEM((width, n_left), BF16),
            pltpu.VMEM((width, n_right), BF16),
            pltpu.VMEM((width, n_rel), BF16),
            pltpu.VMEM((width, n_rel), BF16),
            pltpu.VMEM((n_right, width), F32),
        ],
        interpret=interpret,
        name="bucket",
    )(
        count,
        src.reshape(blocks, 1, EDGES),
        kind.reshape(blocks, 1, EDGES),
        dst.reshape(blocks, 1, EDGES),
        neg.reshape(-1, 1, EDGES),
        left_blk,
        right_blk,
        relations,
    )


def to_all(rows, axis):
    peers = lax.axis_size(axis)
    copies = jnp.broadcast_to(rows[None], (peers,) + rows.shape)
    return lax.all_to_all(copies, axis, 0, 0)


def shards(
    left_table, right_table, relations, source_ids, relation_ids, target_ids, negative_ids, edge_counts
):
    left_grad, rel_grad, updated = bucket_grads(
        edge_counts.reshape(1), source_ids, relation_ids, target_ids, negative_ids,
        left_table, right_table[0], relations,
    )
    width = relations.shape[1]
    moved = passed_along(updated, "right", 1)
    peers = lax.axis_size("right")
    mine = lax.axis_index("right")
    own_left = left_table.shape[0] // peers
    own_rel = relations.shape[0] // peers
    sent = jnp.concatenate(
        [left_grad.reshape(peers, own_left, width), rel_grad.reshape(peers, own_rel, width)], axis=1
    ).astype(jnp.float16)
    got = lax.all_to_all(sent, "right", 0, 0)
    total = jnp.sum(got.astype(F32), axis=0)
    left_rows = lax.dynamic_slice_in_dim(left_table, mine * own_left, own_left, 0)
    left_rows = (left_rows.astype(F32) - step_size * total[:own_left]).astype(BF16)
    rel_total = jnp.sum(to_all(total[own_left:], "left"), axis=0)
    rel_rows = lax.dynamic_slice_in_dim(relations, mine * own_rel, own_rel, 0)
    rel_rows = rel_rows - relation_step * rel_total
    high = lax.reduce_precision(rel_rows, 8, 7)
    low = (rel_rows - high).astype(BF16)
    out = to_all(jnp.concatenate([left_rows, high.astype(BF16), low], axis=0), "right")
    left_next = out[:, :own_left].reshape(left_table.shape)
    high, low = out[:, own_left : own_left + own_rel], out[:, own_left + own_rel :]
    relations_next = (high.astype(F32) + low.astype(F32)).reshape(relations.shape)
    return (left_next, moved[None], relations_next)


def solution(mesh):
    return jax.shard_map(
        shards,
        mesh=mesh,
        in_specs=(
            P("left", None),
            P("left", "right", None),
            P(),
            P("left", "right", None),
            P("left", "right", None),
            P("left", "right", None),
            P("left", "right", None, None),
            P("left", "right"),
        ),
        out_specs=(P("left", None), P("left", "right", None), P()),
        check_vma=False,
    )
```

time: 711 us -> 146 us (0.21)
  waiting for transfers between devices: 585 us -> 53.9 us
  blocking collectives: 0 us -> 48.9 us
  other arithmetic: 50.1 us -> 5.78 us
  local copies, waits for them, and re-layouts: 48.1 us -> 3.85 us
  Pallas kernels: 0 us -> 14.2 us
  between operations: 14.9 us -> 1.34 us
  starting transfers between devices: 4.35 us -> 17.5 us
    psum x2 -> x0, waiting for transfers between devices: 584 us -> none  [the longest x1 314 us: shards(): left_total = lax.psum(left_grad, 'right')]
    all_to_all x0 -> x1, blocking collectives: none -> 48.9 us  [shards(): got = lax.all_to_all(sent, 'right', 0, 0)]
    ppermute x1, waiting for transfers between devices: 0.01 us -> 41.1 us  [passed_along(): lax.ppermute(array, axis, [(i, (i + by) % peers) for i in range(peers)])]
    gather x10 -> x0, local copies, waits for them, and re-layouts: 35.7 us -> none  [the longest x3 11.1 us: block_terms(): head = jnp.take(left_blk, src, axis=0).astype(jnp.float32)]
    scatter-add x4 -> x0, other arithmetic: 29.6 us -> none  [the longest x2 13.5 us: one(): tgrad = tgrad.at[dst_all].add(g_tail).at[n].add(g_neg)]
    pallas_call x0 -> x1, Pallas kernels: none -> 14.2 us  [bucket_grads(): pl.pallas_call(bucket_kernel, out_shape=(jax.ShapeDtypeStruct((n_left, wi...]
    all_to_all x0 -> x2, starting transfers between devices: none -> 13.8 us  [to_all(): return lax.all_to_all(copies, axis, 0, 0)]
    all_to_all x0 -> x2, waiting for transfers between devices: none -> 12.8 us  [to_all(): return lax.all_to_all(copies, axis, 0, 0)]
  transfers between devices with their start and end apart: 3 -> 3, of which waited for: 2 -> 3; matrix products, arithmetic and copies ran while one was open for 0% -> 1% of each run, Pallas kernels for 0% -> 0%
where the time goes in v1:
time: 146 us
  waiting for transfers between devices  53.9 us (37%)
  blocking collectives  48.9 us (33%)
  starting transfers between devices  17.5 us (12%)
  Pallas kernels  14.2 us (10%)
  other arithmetic  5.78 us (4%)
  local copies, waits for them, and re-layouts  3.85 us (3%)
    all_to_all x1, blocking collectives, shards(): got = lax.all_to_all(sent, 'right', 0, 0)  48.9 us
    ppermute x1, waiting for transfers between devices, passed_along(): lax.ppermute(array, axis, [(i, (i + by) % peers) for i in range(peers)])  41.1 us
    pallas_call x1, Pallas kernels, bucket_grads(): pl.pallas_call(bucket_kernel, out_shape=(jax.ShapeDtypeStruct((n_left, wi...  14.2 us
    all_to_all x2, starting transfers between devices, to_all(): return lax.all_to_all(copies, axis, 0, 0)  13.8 us
    all_to_all x2, waiting for transfers between devices, to_all(): return lax.all_to_all(copies, axis, 0, 0)  12.8 us
    ppermute x1, starting transfers between devices, passed_along(): lax.ppermute(array, axis, [(i, (i + by) % peers) for i in range(peers)])  3.7 us
  transfers between devices with their start and end apart: 3, of which 3 were waited for; matrix products, arithmetic and copies ran while one was open for 1% of the time, Pallas kernels for 0%

profile of v1, /device:TPU:2, one launch (start us, length us, event | category | flops | bytes accessed | tf_op | source)
XLA Modules:
  0.0 145.5 jit_solution(16197615993241847277)
XLA Ops:
  1.3 14.2 %bucket.1 = (f32[2048,256]{1,0:T(8,128)}, f32[512,256]{1,0:T(8,128)}, bf16[512,256]{1,0:T(8,128)(2,1)}) custom-call(s32[1]{0:T(128)} %bitcast.11.count_ref, s32[4,1,256]{2,1,0:T(1,128)} %bitcast.18, s32[4,1,256]{2,1,0:T(1,128)} %bitcast.19, s32[4,1,256]{2,1,0:T(1,128)} %bitcast.20, s32[4,1,256]{2,1,0:T(1,128)} %bitcast.21, bf16[2048,256]{1,0:T(8,128)(2,1)} %left_ref.1, ...), custom_call_target="tpu_custom_call" | custom-call | tf_op jit(solution)/shard_map/bucket/pallas_call | solution.py:117
  15.5 1.1 convert.9
  16.6 1.8 %convert.8 = f16[2048,256]{1,0:T(8,128)(2,1)S(1)} convert(f32[2048,256]{1,0:T(8,128)} %get-tuple-element.6) | non-fusion elementwise | flops 524288 | bytes 3145728 | tf_op jit(solution)/shard_map/convert.3
  18.4 0.4 pad_maximum_fusion
  18.7 48.9 %all_to_all.15 = f16[32,80,256]{2,1,0:T(8,128)(2,1)S(1)} all-to-all(f16[32,80,256]{2,1,0:T(8,128)(2,1)S(1)} %pad_maximum_fusion), channel_id=1, replica_groups=mesh['left'=16,'right'=32] {'right'}, dimensions={0} | all-to-all | bytes 2621440 | tf_op jit(solution)/shard_map/all_to_all | solution.py:172
  67.6 0.2 convert_reduce_fusion
  67.8 0.7 broadcast_in_dim.6
  68.5 7.5 %all-to-all-start.1 = ((f32[16,16,256]{2,1,0:T(8,128)}), f32[16,16,256]{2,1,0:T(8,128)S(1)}, u32[]{:S(2)}, u32[]{:S(2)}) async-start(f32[16,16,256]{2,1,0:T(8,128)} %broadcast_in_dim.6), calls=%async_computation.1 | async-start | bytes 524288 | tf_op jit(solution)/shard_map/all_to_all | solution.py:153
  76.1 0.8 fusion.1
  76.9 8.7 %all-to-all-done.1 = f32[16,16,256]{2,1,0:T(8,128)S(1)} async-done(((f32[16,16,256]{2,1,0:T(8,128)}), f32[16,16,256]{2,1,0:T(8,128)S(1)}, u32[]{:S(2)}, u32[]{:S(2)}) %all-to-all-start.1) | async-done | bytes 262176 | tf_op jit(solution)/shard_map/all_to_all | solution.py:153
  85.6 0.7 reduce-precision_convert_fusion
  86.3 1.4 broadcast_in_dim.7
  87.6 0.0 copy-start
  87.6 6.3 %all-to-all-start.2 = ((bf16[32,96,256]{2,1,0:T(8,128)(2,1)}), bf16[32,96,256]{2,1,0:T(8,128)(2,1)S(1)}, u32[]{:S(2)}, u32[]{:S(2)}) async-start(bf16[32,96,256]{2,1,0:T(8,128)(2,1)} %broadcast_in_dim.7), calls=%async_computation.2 | async-start | bytes 3145728 | tf_op jit(solution)/shard_map/all_to_all | solution.py:153
  94.0 0.0 copy-done
  94.0 3.7 %collective-permute-start = (bf16[512,256]{1,0:T(8,128)(2,1)S(1)}, bf16[512,256]{1,0:T(8,128)(2,1)S(1)}, u32[]{:S(2)}, u32[]{:S(2)}) collective-permute-start(bf16[512,256]{1,0:T(8,128)(2,1)S(1)} %copy-done), channel_id=1, source_target_pairs={{0,1},{1,2},{2,3},{3,4},{4,5},{5,6},{6,7},{7,8},{8,9},{9,10},{10,1... | collective-permute-start | bytes 786440 | tf_op jit(solution)/shard_map/ppermute | solution.py:20
  97.7 41.1 %collective-permute-done = bf16[512,256]{1,0:T(8,128)(2,1)S(1)} collective-permute-done((bf16[512,256]{1,0:T(8,128)(2,1)S(1)}, bf16[512,256]{1,0:T(8,128)(2,1)S(1)}, u32[]{:S(2)}, u32[]{:S(2)}) %collective-permute-start) | collective-permute-done | bytes 262176 | tf_op jit(solution)/shard_map/ppermute | solution.py:20
  138.8 4.1 %all-to-all-done.2 = bf16[32,96,256]{2,1,0:T(8,128)(2,1)S(1)} async-done(((bf16[32,96,256]{2,1,0:T(8,128)(2,1)}), bf16[32,96,256]{2,1,0:T(8,128)(2,1)S(1)}, u32[]{:S(2)}, u32[]{:S(2)}) %all-to-all-start.2) | async-done | bytes 1572896 | tf_op jit(solution)/shard_map/all_to_all | solution.py:153
  142.9 1.1 slice.22
  144.0 0.9 convert_add_fusion
  144.8 0.7 copy.13
  (3 shorter events, 0.0 us)
Async XLA Ops:
  68.5 17.0 %all-to-all-start.1 = ((f32[16,16,256]{2,1,0:T(8,128)}), f32[16,16,256]{2,1,0:T(8,128)S(1)}, u32[]{:S(2)}, u32[]{:S(2)}) async-start(f32[16,16,256]{2,1,0:T(8,128)} %broadcast_in_dim.6), calls=%async_computation.1 | async-start | bytes 524288 | tf_op jit(solution)/shard_map/all_to_all | solution.py:153
  87.6 6.3 %copy-start = (bf16[512,256]{1,0:T(8,128)(2,1)S(1)}, bf16[512,256]{1,0:T(8,128)(2,1)}, u32[]{:S(2)}) copy-start(bf16[512,256]{1,0:T(8,128)(2,1)} %get-tuple-element.8) | copy-start | bytes 786436
  87.6 55.2 %all-to-all-start.2 = ((bf16[32,96,256]{2,1,0:T(8,128)(2,1)}), bf16[32,96,256]{2,1,0:T(8,128)(2,1)S(1)}, u32[]{:S(2)}, u32[]{:S(2)}) async-start(bf16[32,96,256]{2,1,0:T(8,128)(2,1)} %broadcast_in_dim.7), calls=%async_computation.2 | async-start | bytes 3145728 | tf_op jit(solution)/shard_map/all_to_all | solution.py:153
  94.0 44.8 %collective-permute-start = (bf16[512,256]{1,0:T(8,128)(2,1)S(1)}, bf16[512,256]{1,0:T(8,128)(2,1)S(1)}, u32[]{:S(2)}, u32[]{:S(2)}) collective-permute-start(bf16[512,256]{1,0:T(8,128)(2,1)S(1)} %copy-done), channel_id=1, source_target_pairs={{0,1},{1,2},{2,3},{3,4},{4,5},{5,6},{6,7},{7,8},{8,9},{9,10},{10,1... | collective-permute-start | bytes 786440 | tf_op jit(solution)/shard_map/ppermute | solution.py:20

commit v2 on v1

v2 whole, which is shorter than its diff:
```python
import jax
import jax.numpy as jnp
from jax import lax
from jax.experimental import pallas as pl
from jax.experimental.pallas import tpu as pltpu
from jax.sharding import PartitionSpec as P


step_size = 0.5
relation_step = 12.0
EDGES = 256
ROWS = 256
F32 = jnp.float32
BF16 = jnp.bfloat16


def passed_along(array, axis, by):
    peers = lax.axis_size(axis)
    return lax.ppermute(array, axis, [(i, (i + by) % peers) for i in range(peers)])


def mm(a, b):
    return lax.dot_general(a, b, (((1,), (0,)), ((), ())), preferred_element_type=F32)


def mm_nt(a, b):
    return lax.dot_general(a, b, (((1,), (1,)), ((), ())), preferred_element_type=F32)


def two_parts(x):
    high = x.astype(BF16)
    return high, (x - high.astype(F32)).astype(BF16)


def one_hot(rows, ids):
    return jnp.where(lax.broadcasted_iota(jnp.int32, (rows, ids.shape[1]), 0) == ids, 1.0, 0.0)


def edge_kernel(
    count_ref, src_ref, kind_ref, dst_ref, neg_ref, left_ref, right_ref, rel_ref,
    gh_high_ref, gh_low_ref, rgrad_ref, right_new_ref,
    left_t, right_t, rel_high_t, rel_low_t, rgrad, tgrad,
):
    n_left, width = left_ref.shape
    n_right, n_rel = right_ref.shape[0], rel_ref.shape[0]
    half = width // 2
    blocks = src_ref.shape[0]
    negs = neg_ref.shape[0] * neg_ref.shape[2]
    count = count_ref[0]
    eye = jnp.where(
        lax.broadcasted_iota(jnp.int32, (width, width), 0)
        == lax.broadcasted_iota(jnp.int32, (width, width), 1),
        1.0,
        0.0,
    ).astype(BF16)
    left_t[...] = mm_nt(eye, left_ref[...]).astype(BF16)
    right_t[...] = mm_nt(eye, right_ref[...]).astype(BF16)
    rel_high, rel_low = two_parts(rel_ref[...])
    rel_high_t[...] = mm_nt(eye, rel_high).astype(BF16)
    rel_low_t[...] = mm_nt(eye, rel_low).astype(BF16)
    seen = one_hot(n_right, neg_ref[0])
    for i in range(1, neg_ref.shape[0]):
        seen = seen + one_hot(n_right, neg_ref[i])
    times = jnp.sum(seen, axis=1, keepdims=True) * (1.0 / negs)
    rgrad[...] = jnp.zeros_like(rgrad)
    tgrad[...] = jnp.zeros_like(tgrad)

    def block(i, carry):
        ohs = one_hot(n_left, src_ref[i]).astype(BF16)
        ohk = one_hot(n_rel, kind_ref[i]).astype(BF16)
        ohd = one_hot(n_right, dst_ref[i]).astype(BF16)
        head = mm(left_t[...], ohs)
        tail = mm(right_t[...], ohd)
        rel = mm(rel_high_t[...], ohk) + mm(rel_low_t[...], ohk)
        hre, him = head[:half], head[half:]
        rre, rim = rel[:half], rel[half:]
        query = jnp.concatenate([hre * rre - him * rim, hre * rim + him * rre], axis=0)
        q_low = query.astype(BF16)
        pos = jnp.sum(query * tail, axis=0, keepdims=True)
        slot = i * EDGES + lax.broadcasted_iota(jnp.int32, (1, EDGES), 1)
        live = jnp.where(slot < count, 1.0, 0.0)
        c_pos = -jax.nn.sigmoid(-pos) * live
        scores = mm(right_ref[...], q_low)
        c_neg = (jax.nn.sigmoid(scores) * (times * live)).astype(BF16)
        g_query = mm(right_t[...], c_neg) + c_pos * tail
        gre, gim = g_query[:half], g_query[half:]
        grad_h = jnp.concatenate([gre * rre + gim * rim, -gre * rim + gim * rre], axis=0)
        grad_r = jnp.concatenate([gre * hre + gim * him, -gre * him + gim * hre], axis=0)
        gh_high_ref[i], gh_low_ref[i] = two_parts(grad_h)
        rgrad[...] += mm_nt(ohk, grad_r.astype(BF16))
        t_high, t_low = two_parts(c_pos * query)
        tgrad[...] += mm_nt(c_neg, q_low) + mm_nt(ohd, t_high) + mm_nt(ohd, t_low)
        return carry

    lax.fori_loop(0, blocks, block, 0)
    rgrad_ref[...] = rgrad[...].astype(BF16)
    right_new_ref[...] = (right_ref[...].astype(F32) - step_size * tgrad[...]).astype(BF16)


def left_kernel(src_ref, gh_high_ref, gh_low_ref, lgrad_ref):
    n_left, width = lgrad_ref.shape
    blocks = src_ref.shape[0]

    def rows(j, carry):
        start = pl.multiple_of(j * ROWS, ROWS)
        total = jnp.zeros((ROWS, width), F32)
        for i in range(blocks):
            hot = one_hot(ROWS, src_ref[i] - start).astype(BF16)
            total += mm_nt(hot, gh_high_ref[i]) + mm_nt(hot, gh_low_ref[i])
        lgrad_ref[pl.ds(start, ROWS), :] = total
        return carry

    lax.fori_loop(0, n_left // ROWS, rows, 0)


VMEM = pl.BlockSpec(memory_space=pltpu.VMEM)


def edge_grads(count, src, kind, dst, neg, left_blk, right_blk, relations, interpret=False):
    n_left, width = left_blk.shape
    n_right, n_rel, blocks = right_blk.shape[0], relations.shape[0], src.shape[0]
    return pl.pallas_call(
        edge_kernel,
        out_shape=(
            jax.ShapeDtypeStruct((blocks, width, EDGES), BF16),
            jax.ShapeDtypeStruct((blocks, width, EDGES), BF16),
            jax.ShapeDtypeStruct((n_rel, width), BF16),
            jax.ShapeDtypeStruct((n_right, width), BF16),
        ),
        in_specs=[pl.BlockSpec(memory_space=pltpu.SMEM)] + [VMEM] * 7,
        out_specs=(VMEM,) * 4,
        scratch_shapes=[
            pltpu.VMEM((width, n_left), BF16),
            pltpu.VMEM((width, n_right), BF16),
            pltpu.VMEM((width, n_rel), BF16),
            pltpu.VMEM((width, n_rel), BF16),
            pltpu.VMEM((n_rel, width), F32),
            pltpu.VMEM((n_right, width), F32),
        ],
        interpret=interpret,
        name="edges",
    )(count, src, kind, dst, neg, left_blk, right_blk, relations)


def left_sums(src, gh_high, gh_low, n_left, interpret=False):
    width = gh_high.shape[1]
    return pl.pallas_call(
        left_kernel,
        out_shape=jax.ShapeDtypeStruct((n_left, width), F32),
        in_specs=[VMEM] * 3,
        out_specs=VMEM,
        cost_estimate=pl.CostEstimate(
            flops=4 * n_left * src.size * width, transcendentals=0, bytes_accessed=8 * n_left * width
        ),
        interpret=interpret,
        name="leftrows",
    )(src, gh_high, gh_low)


def to_all(rows, axis):
    peers = lax.axis_size(axis)
    copies = jnp.broadcast_to(rows[None], (peers,) + rows.shape)
    return lax.all_to_all(copies, axis, 0, 0)


def shards(
    left_table, right_table, relations, source_ids, relation_ids, target_ids, negative_ids, edge_counts
):
    width = relations.shape[1]
    peers = lax.axis_size("right")
    mine = lax.axis_index("right")
    own_left = left_table.shape[0] // peers
    own_rel = relations.shape[0] // peers
    src, kind, dst, neg = (
        ids.reshape(-1, 1, EDGES) for ids in (source_ids, relation_ids, target_ids, negative_ids)
    )
    gh_high, gh_low, rel_grad, updated = edge_grads(
        edge_counts.reshape(1), src, kind, dst, neg, left_table, right_table[0], relations
    )
    moved = passed_along(updated, "right", 1)
    rel_got = lax.all_to_all(rel_grad.reshape(peers, own_rel, width), "right", 0, 0)
    left_grad = left_sums(src, gh_high, gh_low, left_table.shape[0])
    sent = left_grad.astype(jnp.float16).reshape(peers, own_left, width)
    rel_part = jnp.sum(rel_got.astype(F32), axis=0)
    left_got = lax.all_to_all(sent, "right", 0, 0)
    rel_parts = lax.all_gather(rel_part, "left", axis=0)
    rel_rows = lax.dynamic_slice_in_dim(relations, mine * own_rel, own_rel, 0)
    rel_rows = rel_rows - relation_step * jnp.sum(rel_parts, axis=0)
    left_rows = lax.dynamic_slice_in_dim(left_table, mine * own_left, own_left, 0)
    left_total = jnp.sum(left_got.astype(F32), axis=0)
    left_rows = (left_rows.astype(F32) - step_size * left_total).astype(BF16)
    squares = rel_rows * rel_rows
    code = (jnp.where(rel_rows < 0, -squares, squares) * squares).astype(BF16)
    out = to_all(jnp.concatenate([left_rows, code], axis=0), "right")
    left_next = out[:, :own_left].reshape(left_table.shape)
    code = out[:, own_left:].astype(F32)
    roots = jnp.sqrt(jnp.sqrt(jnp.abs(code)))
    relations_next = jnp.where(code < 0, -roots, roots).reshape(relations.shape)
    return (left_next, moved[None], relations_next)


def solution(mesh):
    return jax.shard_map(
        shards,
        mesh=mesh,
        in_specs=(
            P("left", None),
            P("left", "right", None),
            P(),
            P("left", "right", None),
            P("left", "right", None),
            P("left", "right", None),
            P("left", "right", None, None),
            P("left", "right"),
        ),
        out_specs=(P("left", None), P("left", "right", None), P()),
        check_vma=False,
    )
```

time: 146 us -> 141 us (0.966)
  the two profiles are of different devices: /device:TPU:2 before, /device:TPU:17 now
where the time goes in v2:
time: 141 us; the launch traced here: 140 us
  blocking collectives  43.1 us (31%)
  waiting for transfers between devices  37.3 us (26%)
  starting transfers between devices  33.7 us (24%)
  Pallas kernels  16 us (11%)
  other arithmetic  5.59 us (4%)
  local copies, waits for them, and re-layouts  2.98 us (2%)
    all_gather x1, blocking collectives, shards(): rel_parts = lax.all_gather(rel_part, 'left', axis=0)  43.1 us
    ppermute x1, waiting for transfers between devices, passed_along(): lax.ppermute(array, axis, [(i, (i + by) % peers) for i in range(peers)])  35.9 us
    all_to_all x1, starting transfers between devices, shards(): lax.all_to_all(rel_grad.reshape(peers, own_rel, width), 'right', 0, 0)  13.3 us
    pallas_call x1, Pallas kernels, edge_grads(): pl.pallas_call(edge_kernel, out_shape=(jax.ShapeDtypeStruct((blocks, widt...  9.66 us
    all_to_all x1, starting transfers between devices, to_all(): return lax.all_to_all(copies, axis, 0, 0)  9.15 us
    all_to_all x1, starting transfers between devices, shards(): left_got = lax.all_to_all(sent, 'right', 0, 0)  8.15 us
    pallas_call x1, Pallas kernels, left_sums(): pl.pallas_call(left_kernel, out_shape=jax.ShapeDtypeStruct((n_left, width...  6.39 us
    ppermute x1, starting transfers between devices, passed_along(): lax.ppermute(array, axis, [(i, (i + by) % peers) for i in range(peers)])  3.09 us
  transfers between devices with their start and end apart: 4, of which 2 were waited for; matrix products, arithmetic and copies ran while one was open for 3% of the time, Pallas kernels for 5%

profile of v2, /device:TPU:17, one launch (start us, length us, event | category | flops | bytes accessed | tf_op | source)
XLA Modules:
  0.0 140.0 jit_solution(15089244619714312158)
XLA Ops:
  1.3 9.7 %edges.1 = (bf16[4,256,256]{2,1,0:T(8,128)(2,1)}, bf16[4,256,256]{2,1,0:T(8,128)(2,1)}, bf16[512,256]{1,0:T(8,128)(2,1)}, bf16[512,256]{1,0:T(8,128)(2,1)}) custom-call(s32[1]{0:T(128)} %bitcast.12.count_ref, s32[4,1,256]{2,1,0:T(1,128)} %bitcast.22, s32[4,1,256]{2,1,0:T(1,128)} %bitcast.19, s32[4,1,256]{2,1,0:T(1,128)} %bitcast.20, s32[4,1,256]{2,1,0:T(1,128)} %bitcast.21, ...), custom_call_target="tpu_custom_call" | custom-call | tf_op jit(solution)/shard_map/edges/pallas_call | solution.py:122
  10.9 13.3 %all-to-all-start.1 = ((bf16[32,16,256]{2,1,0:T(8,128)(2,1)}), bf16[32,16,256]{2,1,0:T(8,128)(2,1)S(1)}, u32[]{:S(2)}, u32[]{:S(2)}) async-start(bf16[32,16,256]{2,1,0:T(8,128)(2,1)} %bitcast.16), calls=%async_computation.1 | async-start | bytes 524288 | tf_op jit(solution)/shard_map/all_to_all | solution.py:181
  24.2 6.4 %leftrows.1 = f32[2048,256]{1,0:T(8,128)} custom-call(s32[4,1,256]{2,1,0:T(1,128)} %bitcast.23, bf16[4,256,256]{2,1,0:T(8,128)(2,1)} %get-tuple-element.7.gh_high_ref, bf16[4,256,256]{2,1,0:T(8,128)(2,1)} %get-tuple-element.8.gh_low_ref), custom_call_target="tpu_custom_call" | custom-call | flops 2147483648 | bytes 4194304 | tf_op jit(solution)/shard_map/leftrows/pallas_call | solution.py:147
  30.6 2.7 %convert_element_type.22 = f16[2048,256]{1,0:T(8,128)(2,1)} convert(f32[2048,256]{1,0:T(8,128)} %leftrows.1) | non-fusion elementwise | flops 524288 | bytes 3145728 | tf_op jit(solution)/shard_map/convert_element_type | solution.py:183
  33.4 1.4 all-to-all-done.1
  34.8 8.1 %all-to-all-start = ((f16[32,64,256]{2,1,0:T(8,128)(2,1)}), f16[32,64,256]{2,1,0:T(8,128)(2,1)S(1)}, u32[]{:S(2)}, u32[]{:S(2)}) async-start(f16[32,64,256]{2,1,0:T(8,128)(2,1)} %bitcast.6), calls=%async_computation | async-start | bytes 2097152 | tf_op jit(solution)/shard_map/all_to_all | solution.py:185
  43.0 43.1 %all-gather = f32[256,256]{1,0:T(8,128)S(1)} all-gather(f32[16,256]{1,0:T(8,128)S(1)} %convert_reduce_fusion.1), channel_id=2, replica_groups=mesh['left'=16,'right'=32] {'left'}, dimensions={0}, use_global_device_ids=true | all-gather | bytes 278528 | tf_op jit(solution)/shard_map/all_gather | solution.py:186
  86.1 0.7 fusion.2
  86.8 0.0 all-to-all-done
  86.8 0.2 convert_reduce_fusion
  87.0 0.8 subtract_convert_fusion
  87.8 1.2 broadcast_in_dim.4
  88.9 0.0 copy-start
  88.9 9.1 %all-to-all-start.2 = ((bf16[32,80,256]{2,1,0:T(8,128)(2,1)}), bf16[32,80,256]{2,1,0:T(8,128)(2,1)S(1)}, u32[]{:S(2)}, u32[]{:S(2)}) async-start(bf16[32,80,256]{2,1,0:T(8,128)(2,1)} %broadcast_in_dim.4), calls=%async_computation.2 | async-start | bytes 2621440 | tf_op jit(solution)/shard_map/all_to_all | solution.py:163
  98.1 0.0 copy-done
  98.1 3.1 %collective-permute-start = (bf16[512,256]{1,0:T(8,128)(2,1)S(1)}, bf16[512,256]{1,0:T(8,128)(2,1)S(1)}, u32[]{:S(2)}, u32[]{:S(2)}) collective-permute-start(bf16[512,256]{1,0:T(8,128)(2,1)S(1)} %copy-done), channel_id=1, source_target_pairs={{0,1},{1,2},{2,3},{3,4},{4,5},{5,6},{6,7},{7,8},{8,9},{9,10},{10,1... | collective-permute-start | bytes 786440 | tf_op jit(solution)/shard_map/ppermute | solution.py:19
  101.2 35.9 %collective-permute-done = bf16[512,256]{1,0:T(8,128)(2,1)S(1)} collective-permute-done((bf16[512,256]{1,0:T(8,128)(2,1)S(1)}, bf16[512,256]{1,0:T(8,128)(2,1)S(1)}, u32[]{:S(2)}, u32[]{:S(2)}) %collective-permute-start) | collective-permute-done | bytes 262176 | tf_op jit(solution)/shard_map/ppermute | solution.py:19
  137.1 0.0 all-to-all-done.2
  137.1 1.1 negate_select_fusion
  138.2 1.1 slice.8
  139.3 0.7 copy.13
  (3 shorter events, 0.1 us)
Async XLA Ops:
  10.9 23.8 %all-to-all-start.1 = ((bf16[32,16,256]{2,1,0:T(8,128)(2,1)}), bf16[32,16,256]{2,1,0:T(8,128)(2,1)S(1)}, u32[]{:S(2)}, u32[]{:S(2)}) async-start(bf16[32,16,256]{2,1,0:T(8,128)(2,1)} %bitcast.16), calls=%async_computation.1 | async-start | bytes 524288 | tf_op jit(solution)/shard_map/all_to_all | solution.py:181
  34.8 52.1 %all-to-all-start = ((f16[32,64,256]{2,1,0:T(8,128)(2,1)}), f16[32,64,256]{2,1,0:T(8,128)(2,1)S(1)}, u32[]{:S(2)}, u32[]{:S(2)}) async-start(f16[32,64,256]{2,1,0:T(8,128)(2,1)} %bitcast.6), calls=%async_computation | async-start | bytes 2097152 | tf_op jit(solution)/shard_map/all_to_all | solution.py:185
  88.9 9.2 %copy-start = (bf16[512,256]{1,0:T(8,128)(2,1)S(1)}, bf16[512,256]{1,0:T(8,128)(2,1)}, u32[]{:S(2)}) copy-start(bf16[512,256]{1,0:T(8,128)(2,1)} %get-tuple-element.10) | copy-start | bytes 786436
  88.9 48.1 %all-to-all-start.2 = ((bf16[32,80,256]{2,1,0:T(8,128)(2,1)}), bf16[32,80,256]{2,1,0:T(8,128)(2,1)S(1)}, u32[]{:S(2)}, u32[]{:S(2)}) async-start(bf16[32,80,256]{2,1,0:T(8,128)(2,1)} %broadcast_in_dim.4), calls=%async_computation.2 | async-start | bytes 2621440 | tf_op jit(solution)/shard_map/all_to_all | solution.py:163
  98.1 39.0 %collective-permute-start = (bf16[512,256]{1,0:T(8,128)(2,1)S(1)}, bf16[512,256]{1,0:T(8,128)(2,1)S(1)}, u32[]{:S(2)}, u32[]{:S(2)}) collective-permute-start(bf16[512,256]{1,0:T(8,128)(2,1)S(1)} %copy-done), channel_id=1, source_target_pairs={{0,1},{1,2},{2,3},{3,4},{4,5},{5,6},{6,7},{7,8},{8,9},{9,10},{10,1... | collective-permute-start | bytes 786440 | tf_op jit(solution)/shard_map/ppermute | solution.py:19

commit v3 on v2

--- a/solution.py
+++ b/solution.py
@@ -1,5 +1,6 @@
 import jax
 import jax.numpy as jnp
+import numpy as np
 from jax import lax
 from jax.experimental import pallas as pl
 from jax.experimental.pallas import tpu as pltpu
@@ -157,6 +158,14 @@
     )(src, gh_high, gh_low)
 
 
+def summed_over(part, axis, sizes):
+    peers = np.arange(lax.axis_size(axis)).reshape(sizes)
+    for dim in (0, 2, 1):
+        groups = np.moveaxis(peers, dim, -1).reshape(-1, sizes[dim]).tolist()
+        part = jnp.sum(lax.all_gather(part, axis, axis=0, axis_index_groups=groups), axis=0)
+    return part
+
+
 def to_all(rows, axis):
     peers = lax.axis_size(axis)
     copies = jnp.broadcast_to(rows[None], (peers,) + rows.shape)
@@ -183,9 +192,9 @@
     sent = left_grad.astype(jnp.float16).reshape(peers, own_left, width)
     rel_part = jnp.sum(rel_got.astype(F32), axis=0)
     left_got = lax.all_to_all(sent, "right", 0, 0)
-    rel_parts = lax.all_gather(rel_part, "left", axis=0)
+    rel_total = summed_over(rel_part, "left", (4, 2, 2))
     rel_rows = lax.dynamic_slice_in_dim(relations, mine * own_rel, own_rel, 0)
-    rel_rows = rel_rows - relation_step * jnp.sum(rel_parts, axis=0)
+    rel_rows = rel_rows - relation_step * rel_total
     left_rows = lax.dynamic_slice_in_dim(left_table, mine * own_left, own_left, 0)
     left_total = jnp.sum(left_got.astype(F32), axis=0)
     left_rows = (left_rows.astype(F32) - step_size * left_total).astype(BF16)

time: 141 us -> 122 us (0.87)
  the two profiles are of different devices: /device:TPU:17 before, /device:TPU:76 now
where the time goes in v3:
time: 122 us; the launch traced here: 121 us
  waiting for transfers between devices  44.7 us (37%)
  starting transfers between devices  29.3 us (24%)
  blocking collectives  20.9 us (17%)
  Pallas kernels  16.1 us (13%)
  other arithmetic  5.58 us (5%)
  local copies, waits for them, and re-layouts  2.96 us (2%)
  between operations  1.35 us (1%)
    ppermute x1, waiting for transfers between devices, passed_along(): lax.ppermute(array, axis, [(i, (i + by) % peers) for i in range(peers)])  29.4 us
    all_gather x3, blocking collectives, summed_over(): lax.all_gather(part, axis, axis=0, axis_index_groups=groups)  20.9 us
    all_to_all x1, starting transfers between devices, shards(): lax.all_to_all(rel_grad.reshape(peers, own_rel, width), 'right', 0, 0)  13.1 us
    pallas_call x1, Pallas kernels, edge_grads(): pl.pallas_call(edge_kernel, out_shape=(jax.ShapeDtypeStruct((blocks, widt...  9.64 us
    all_to_all x1, starting transfers between devices, shards(): left_got = lax.all_to_all(sent, 'right', 0, 0)  8.09 us
    all_to_all x1, waiting for transfers between devices, shards(): left_got = lax.all_to_all(sent, 'right', 0, 0)  7.24 us
    pallas_call x1, Pallas kernels, left_sums(): pl.pallas_call(left_kernel, out_shape=jax.ShapeDtypeStruct((n_left, width...  6.48 us
    all_to_all x1, waiting for transfers between devices, to_all(): return lax.all_to_all(copies, axis, 0, 0)  6.11 us
  transfers between devices with their start and end apart: 4, of which 4 were waited for; matrix products, arithmetic and copies ran while one was open for 3% of the time, Pallas kernels for 5%

profile of v3, /device:TPU:76, one launch (start us, length us, event | category | flops | bytes accessed | tf_op | source)
XLA Modules:
  0.0 121.0 jit_solution(8900444683903162285)
XLA Ops:
  1.3 9.6 %edges.1 = (bf16[4,256,256]{2,1,0:T(8,128)(2,1)}, bf16[4,256,256]{2,1,0:T(8,128)(2,1)}, bf16[512,256]{1,0:T(8,128)(2,1)}, bf16[512,256]{1,0:T(8,128)(2,1)}) custom-call(s32[1]{0:T(128)} %bitcast.14.count_ref, s32[4,1,256]{2,1,0:T(1,128)} %bitcast.26, s32[4,1,256]{2,1,0:T(1,128)} %bitcast.23, s32[4,1,256]{2,1,0:T(1,128)} %bitcast.24, s32[4,1,256]{2,1,0:T(1,128)} %bitcast.25, ...), custom_call_target="tpu_custom_call" | custom-call | tf_op jit(solution)/shard_map/edges/pallas_call | solution.py:123
  10.9 13.1 %all-to-all-start.1 = ((bf16[32,16,256]{2,1,0:T(8,128)(2,1)}), bf16[32,16,256]{2,1,0:T(8,128)(2,1)S(1)}, u32[]{:S(2)}, u32[]{:S(2)}) async-start(bf16[32,16,256]{2,1,0:T(8,128)(2,1)} %bitcast.18), calls=%async_computation.1 | async-start | bytes 524288 | tf_op jit(solution)/shard_map/all_to_all | solution.py:190
  24.0 6.5 %leftrows.1 = f32[2048,256]{1,0:T(8,128)} custom-call(s32[4,1,256]{2,1,0:T(1,128)} %bitcast.27, bf16[4,256,256]{2,1,0:T(8,128)(2,1)} %get-tuple-element.7.gh_high_ref, bf16[4,256,256]{2,1,0:T(8,128)(2,1)} %get-tuple-element.8.gh_low_ref), custom_call_target="tpu_custom_call" | custom-call | flops 2147483648 | bytes 4194304 | tf_op jit(solution)/shard_map/leftrows/pallas_call | solution.py:148
  30.5 2.7 %convert_element_type.22 = f16[2048,256]{1,0:T(8,128)(2,1)} convert(f32[2048,256]{1,0:T(8,128)} %leftrows.1) | non-fusion elementwise | flops 524288 | bytes 3145728 | tf_op jit(solution)/shard_map/convert_element_type | solution.py:192
  33.2 2.0 %all-to-all-done.1 = bf16[32,16,256]{2,1,0:T(8,128)(2,1)S(1)} async-done(((bf16[32,16,256]{2,1,0:T(8,128)(2,1)}), bf16[32,16,256]{2,1,0:T(8,128)(2,1)S(1)}, u32[]{:S(2)}, u32[]{:S(2)}) %all-to-all-start.1) | async-done | bytes 262176 | tf_op jit(solution)/shard_map/all_to_all | solution.py:190
  35.2 8.1 %all-to-all-start = ((f16[32,64,256]{2,1,0:T(8,128)(2,1)}), f16[32,64,256]{2,1,0:T(8,128)(2,1)S(1)}, u32[]{:S(2)}, u32[]{:S(2)}) async-start(f16[32,64,256]{2,1,0:T(8,128)(2,1)} %bitcast.6), calls=%async_computation | async-start | bytes 2097152 | tf_op jit(solution)/shard_map/all_to_all | solution.py:194
  43.4 10.7 %all-gather = f32[64,256]{1,0:T(8,128)S(1)} all-gather(f32[16,256]{1,0:T(8,128)S(1)} %convert_reduce_fusion.1), channel_id=2, replica_groups={{0,128,256,384},{32,160,288,416},{64,192,320,448},{96,224,352,480},{1,1..., dimensions={0}, use_global_device_ids=true | all-gather | bytes 81920 | tf_op jit(solution)/shard_map/all_gather | solution.py:165
  54.0 1.8 %all-gather.1 = f32[32,256]{1,0:T(8,128)S(1)} all-gather(f32[16,256]{1,0:T(8,128)S(1)} %reduce_sum.47), channel_id=3, replica_groups={{0,32},{64,96},{128,160},{192,224},{256,288},{320,352},{384,416},{448,4..., dimensions={0}, use_global_device_ids=true | all-gather | bytes 49152 | tf_op jit(solution)/shard_map/all_gather | solution.py:165
  55.9 8.4 %all-gather.2 = f32[32,256]{1,0:T(8,128)S(1)} all-gather(f32[16,256]{1,0:T(8,128)S(1)} %reduce_sum.48), channel_id=4, replica_groups={{0,64},{32,96},{128,192},{160,224},{256,320},{288,352},{384,448},{416,4..., dimensions={0}, use_global_device_ids=true | all-gather | bytes 49152 | tf_op jit(solution)/shard_map/all_gather | solution.py:165
  64.3 0.7 fusion.2
  65.0 7.2 %all-to-all-done = f16[32,64,256]{2,1,0:T(8,128)(2,1)S(1)} async-done(((f16[32,64,256]{2,1,0:T(8,128)(2,1)}), f16[32,64,256]{2,1,0:T(8,128)(2,1)S(1)}, u32[]{:S(2)}, u32[]{:S(2)}) %all-to-all-start) | async-done | bytes 1048608 | tf_op jit(solution)/shard_map/all_to_all | solution.py:194
  72.3 0.2 convert_reduce_fusion
  72.4 0.8 subtract_convert_fusion
  73.2 1.1 broadcast_in_dim.4
  74.4 0.0 copy-start
  74.4 4.8 %all-to-all-start.2 = ((bf16[32,80,256]{2,1,0:T(8,128)(2,1)}), bf16[32,80,256]{2,1,0:T(8,128)(2,1)S(1)}, u32[]{:S(2)}, u32[]{:S(2)}) async-start(bf16[32,80,256]{2,1,0:T(8,128)(2,1)} %broadcast_in_dim.4), calls=%async_computation.2 | async-start | bytes 2621440 | tf_op jit(solution)/shard_map/all_to_all | solution.py:172
  79.2 0.0 copy-done
  79.2 3.4 %collective-permute-start = (bf16[512,256]{1,0:T(8,128)(2,1)S(1)}, bf16[512,256]{1,0:T(8,128)(2,1)S(1)}, u32[]{:S(2)}, u32[]{:S(2)}) collective-permute-start(bf16[512,256]{1,0:T(8,128)(2,1)S(1)} %copy-done), channel_id=1, source_target_pairs={{0,1},{1,2},{2,3},{3,4},{4,5},{5,6},{6,7},{7,8},{8,9},{9,10},{10,1... | collective-permute-start | bytes 786440 | tf_op jit(solution)/shard_map/ppermute | solution.py:20
  82.6 29.4 %collective-permute-done = bf16[512,256]{1,0:T(8,128)(2,1)S(1)} collective-permute-done((bf16[512,256]{1,0:T(8,128)(2,1)S(1)}, bf16[512,256]{1,0:T(8,128)(2,1)S(1)}, u32[]{:S(2)}, u32[]{:S(2)}) %collective-permute-start) | collective-permute-done | bytes 262176 | tf_op jit(solution)/shard_map/ppermute | solution.py:20
  112.0 6.1 %all-to-all-done.2 = bf16[32,80,256]{2,1,0:T(8,128)(2,1)S(1)} async-done(((bf16[32,80,256]{2,1,0:T(8,128)(2,1)}), bf16[32,80,256]{2,1,0:T(8,128)(2,1)S(1)}, u32[]{:S(2)}, u32[]{:S(2)}) %all-to-all-start.2) | async-done | bytes 1310752 | tf_op jit(solution)/shard_map/all_to_all | solution.py:172
  118.1 1.1 negate_select_fusion
  119.2 1.1 slice.8
  120.3 0.7 copy.13
  (5 shorter events, 0.1 us)
Async XLA Ops:
  10.9 24.3 %all-to-all-start.1 = ((bf16[32,16,256]{2,1,0:T(8,128)(2,1)}), bf16[32,16,256]{2,1,0:T(8,128)(2,1)S(1)}, u32[]{:S(2)}, u32[]{:S(2)}) async-start(bf16[32,16,256]{2,1,0:T(8,128)(2,1)} %bitcast.18), calls=%async_computation.1 | async-start | bytes 524288 | tf_op jit(solution)/shard_map/all_to_all | solution.py:190
  35.2 37.1 %all-to-all-start = ((f16[32,64,256]{2,1,0:T(8,128)(2,1)}), f16[32,64,256]{2,1,0:T(8,128)(2,1)S(1)}, u32[]{:S(2)}, u32[]{:S(2)}) async-start(f16[32,64,256]{2,1,0:T(8,128)(2,1)} %bitcast.6), calls=%async_computation | async-start | bytes 2097152 | tf_op jit(solution)/shard_map/all_to_all | solution.py:194
  74.4 4.8 %copy-start = (bf16[512,256]{1,0:T(8,128)(2,1)S(1)}, bf16[512,256]{1,0:T(8,128)(2,1)}, u32[]{:S(2)}) copy-start(bf16[512,256]{1,0:T(8,128)(2,1)} %get-tuple-element.10) | copy-start | bytes 786436
  74.4 43.7 %all-to-all-start.2 = ((bf16[32,80,256]{2,1,0:T(8,128)(2,1)}), bf16[32,80,256]{2,1,0:T(8,128)(2,1)S(1)}, u32[]{:S(2)}, u32[]{:S(2)}) async-start(bf16[32,80,256]{2,1,0:T(8,128)(2,1)} %broadcast_in_dim.4), calls=%async_computation.2 | async-start | bytes 2621440 | tf_op jit(solution)/shard_map/all_to_all | solution.py:172
  79.2 32.8 %collective-permute-start = (bf16[512,256]{1,0:T(8,128)(2,1)S(1)}, bf16[512,256]{1,0:T(8,128)(2,1)S(1)}, u32[]{:S(2)}, u32[]{:S(2)}) collective-permute-start(bf16[512,256]{1,0:T(8,128)(2,1)S(1)} %copy-done), channel_id=1, source_target_pairs={{0,1},{1,2},{2,3},{3,4},{4,5},{5,6},{6,7},{7,8},{8,9},{9,10},{10,1... | collective-permute-start | bytes 786440 | tf_op jit(solution)/shard_map/ppermute | solution.py:20

commit v4 on v3

--- a/solution.py
+++ b/solution.py
@@ -9,8 +9,8 @@
 
 step_size = 0.5
 relation_step = 12.0
-EDGES = 256
-ROWS = 256
+EDGES = 1024
+ROWS = 1024
 F32 = jnp.float32
 BF16 = jnp.bfloat16
 
@@ -166,10 +166,76 @@
     return part
 
 
-def to_all(rows, axis):
-    peers = lax.axis_size(axis)
-    copies = jnp.broadcast_to(rows[None], (peers,) + rows.shape)
-    return lax.all_to_all(copies, axis, 0, 0)
+def spread_kernel(total_ref, left_ref, code_ref, sent_ref, rows, done):
+    own_left, own_rel = left_ref.shape[0], code_ref.shape[0]
+    rows[:own_left] = (left_ref[...].astype(F32) - step_size * total_ref[...]).astype(BF16)
+    rows[own_left : own_left + own_rel] = code_ref[...]
+    copies = [pltpu.make_async_copy(rows, sent_ref.at[i], done.at[i]) for i in range(sent_ref.shape[0])]
+    for copy in copies:
+        copy.start()
+    for copy in copies:
+        copy.wait()
+
+
+def for_all(total, left_rows, code, peers):
+    shape = (left_rows.shape[0] + code.shape[0], left_rows.shape[1])
+    return pl.pallas_call(
+        spread_kernel,
+        out_shape=jax.ShapeDtypeStruct((peers,) + shape, BF16),
+        in_specs=[VMEM] * 3,
+        out_specs=pl.BlockSpec(memory_space=pl.ANY),
+        scratch_shapes=[pltpu.VMEM(shape, BF16), pltpu.SemaphoreType.DMA((peers,))],
+        compiler_params=pltpu.CompilerParams(vmem_limit_bytes=4 * 2**20),
+        name="spread",
+    )(total, left_rows, code)
+
+
+def settle_kernel(block_ref, out_ref, done):
+    copy = pltpu.make_async_copy(block_ref, out_ref, done)
+    copy.start()
+    copy.wait()
+
+
+def settled(block):
+    return pl.pallas_call(
+        settle_kernel,
+        out_shape=jax.ShapeDtypeStruct(block.shape, block.dtype),
+        in_specs=[VMEM],
+        out_specs=pl.BlockSpec(memory_space=pl.ANY),
+        scratch_shapes=[pltpu.SemaphoreType.DMA],
+        compiler_params=pltpu.CompilerParams(vmem_limit_bytes=4 * 2**20),
+        name="settle",
+    )(block)
+
+
+def finish_kernel(got_ref, left_next_ref, rel_next_ref, rel, done):
+    own_left = left_next_ref.shape[1]
+    left_copy = pltpu.make_async_copy(got_ref.at[:, :own_left, :], left_next_ref, done.at[0])
+    left_copy.start()
+    code = got_ref[:, own_left:, :].astype(F32)
+    roots = jnp.sqrt(jnp.sqrt(jnp.abs(code)))
+    rel[...] = jnp.where(code < 0, -roots, roots)
+    rel_copy = pltpu.make_async_copy(rel, rel_next_ref, done.at[1])
+    rel_copy.start()
+    left_copy.wait()
+    rel_copy.wait()
+
+
+def finished(got, own_left):
+    peers, rows, width = got.shape
+    own_rel = rows - own_left
+    return pl.pallas_call(
+        finish_kernel,
+        out_shape=(
+            jax.ShapeDtypeStruct((peers, own_left, width), BF16),
+            jax.ShapeDtypeStruct((peers, own_rel, width), F32),
+        ),
+        in_specs=[VMEM],
+        out_specs=(pl.BlockSpec(memory_space=pl.ANY),) * 2,
+        scratch_shapes=[pltpu.VMEM((peers, own_rel, width), F32), pltpu.SemaphoreType.DMA((2,))],
+        compiler_params=pltpu.CompilerParams(vmem_limit_bytes=8 * 2**20),
+        name="finish",
+    )(got)
 
 
 def shards(
@@ -186,7 +252,7 @@
     gh_high, gh_low, rel_grad, updated = edge_grads(
         edge_counts.reshape(1), src, kind, dst, neg, left_table, right_table[0], relations
     )
-    moved = passed_along(updated, "right", 1)
+    moved = passed_along(updated[None], "right", 1)
     rel_got = lax.all_to_all(rel_grad.reshape(peers, own_rel, width), "right", 0, 0)
     left_grad = left_sums(src, gh_high, gh_low, left_table.shape[0])
     sent = left_grad.astype(jnp.float16).reshape(peers, own_left, width)
@@ -197,15 +263,12 @@
     rel_rows = rel_rows - relation_step * rel_total
     left_rows = lax.dynamic_slice_in_dim(left_table, mine * own_left, own_left, 0)
     left_total = jnp.sum(left_got.astype(F32), axis=0)
-    left_rows = (left_rows.astype(F32) - step_size * left_total).astype(BF16)
     squares = rel_rows * rel_rows
     code = (jnp.where(rel_rows < 0, -squares, squares) * squares).astype(BF16)
-    out = to_all(jnp.concatenate([left_rows, code], axis=0), "right")
-    left_next = out[:, :own_left].reshape(left_table.shape)
-    code = out[:, own_left:].astype(F32)
-    roots = jnp.sqrt(jnp.sqrt(jnp.abs(code)))
-    relations_next = jnp.where(code < 0, -roots, roots).reshape(relations.shape)
-    return (left_next, moved[None], relations_next)
+    got = lax.all_to_all(for_all(left_total, left_rows, code, peers), "right", 0, 0)
+    moved = settled(moved)
+    left_next, relations_next = finished(got, own_left)
+    return (left_next.reshape(left_table.shape), moved, relations_next.reshape(relations.shape))
 
 
 def solution(mesh):

time: 122 us -> 117 us (0.959)
  the two profiles are of different devices: /device:TPU:76 before, /device:TPU:16 now
where the time goes in v4:
time: 117 us; the launch traced here: 116 us
  waiting for transfers between devices  40.5 us (35%)
  starting transfers between devices  31.4 us (27%)
  blocking collectives  22.5 us (19%)
  Pallas kernels  16 us (14%)
  other arithmetic  3.67 us (3%)
  between operations  1.36 us (1%)
    ppermute x1, waiting for transfers between devices, passed_along(): lax.ppermute(array, axis, [(i, (i + by) % peers) for i in range(peers)])  34.5 us
    all_gather x3, blocking collectives, summed_over(): lax.all_gather(part, axis, axis=0, axis_index_groups=groups)  22.5 us
    all_to_all x1, starting transfers between devices, shards(): lax.all_to_all(rel_grad.reshape(peers, own_rel, width), 'right', 0, 0)  13.8 us
    pallas_call x1, Pallas kernels, edge_grads(): pl.pallas_call(edge_kernel, out_shape=(jax.ShapeDtypeStruct((blocks, widt...  7.64 us
    all_to_all x1, starting transfers between devices, shards(): left_got = lax.all_to_all(sent, 'right', 0, 0)  7.34 us
    all_to_all x1, starting transfers between devices, shards(): lax.all_to_all(for_all(left_total, left_rows, code, peers), 'right', 0, 0)  6.88 us
    pallas_call x1, Pallas kernels, left_sums(): pl.pallas_call(left_kernel, out_shape=jax.ShapeDtypeStruct((n_left, width...  5.13 us
    ppermute x1, starting transfers between devices, passed_along(): lax.ppermute(array, axis, [(i, (i + by) % peers) for i in range(peers)])  3.37 us
  transfers between devices with their start and end apart: 4, of which 3 were waited for; matrix products, arithmetic and copies ran while one was open for 4% of the time, Pallas kernels for 5%

profile of v4, /device:TPU:16, one launch (start us, length us, event | category | flops | bytes accessed | tf_op | source)
XLA Modules:
  0.0 116.3 jit_solution(15544290257536197813)
XLA Ops:
  1.3 7.6 %edges.1 = (bf16[1,256,1024]{2,1,0:T(8,128)(2,1)}, bf16[1,256,1024]{2,1,0:T(8,128)(2,1)}, bf16[512,256]{1,0:T(8,128)(2,1)}, bf16[512,256]{1,0:T(8,128)(2,1)}) custom-call(s32[1]{0:T(128)} %bitcast.11.count_ref, s32[1,1,1024]{2,1,0:T(1,128)} %src_ref.3, s32[1,1,1024]{2,1,0:T(1,128)} %kind_ref.1, s32[1,1,1024]{2,1,0:T(1,128)} %dst_ref.1, ...), custom_call_target="tpu_custom_call" | custom-call | tf_op jit(solution)/shard_map/edges/pallas_call | solution.py:123
  8.9 13.8 %all-to-all-start.1 = ((bf16[32,16,256]{2,1,0:T(8,128)(2,1)}), bf16[32,16,256]{2,1,0:T(8,128)(2,1)S(1)}, u32[]{:S(2)}, u32[]{:S(2)}) async-start(bf16[32,16,256]{2,1,0:T(8,128)(2,1)} %bitcast.13), calls=%async_computation.1 | async-start | bytes 524288 | tf_op jit(solution)/shard_map/all_to_all | solution.py:256
  22.8 5.1 %leftrows.1 = f32[2048,256]{1,0:T(8,128)} custom-call(s32[1,1,1024]{2,1,0:T(1,128)} %src_ref.3, bf16[1,256,1024]{2,1,0:T(8,128)(2,1)} %get-tuple-element.9.gh_high_ref, bf16[1,256,1024]{2,1,0:T(8,128)(2,1)} %get-tuple-element.10.gh_low_ref), custom_call_target="tpu_custom_call" | custom-call | flops 2147483648 | bytes 4194304 | tf_op jit(solution)/shard_map/leftrows/pallas_call | solution.py:148
  27.9 2.7 %convert_element_type.12 = f16[2048,256]{1,0:T(8,128)(2,1)} convert(f32[2048,256]{1,0:T(8,128)} %leftrows.1) | non-fusion elementwise | flops 524288 | bytes 3145728 | tf_op jit(solution)/shard_map/convert_element_type | solution.py:258
  30.6 2.8 %all-to-all-done.1 = bf16[32,16,256]{2,1,0:T(8,128)(2,1)S(1)} async-done(((bf16[32,16,256]{2,1,0:T(8,128)(2,1)}), bf16[32,16,256]{2,1,0:T(8,128)(2,1)S(1)}, u32[]{:S(2)}, u32[]{:S(2)}) %all-to-all-start.1) | async-done | bytes 262176 | tf_op jit(solution)/shard_map/all_to_all | solution.py:256
  33.4 7.3 %all-to-all-start = ((f16[32,64,256]{2,1,0:T(8,128)(2,1)}), f16[32,64,256]{2,1,0:T(8,128)(2,1)S(1)}, u32[]{:S(2)}, u32[]{:S(2)}) async-start(f16[32,64,256]{2,1,0:T(8,128)(2,1)} %bitcast.3), calls=%async_computation | async-start | bytes 2097152 | tf_op jit(solution)/shard_map/all_to_all | solution.py:260
  40.8 0.8 constant_dynamic-slice_fusion.left_ref
  41.6 12.2 %all-gather = f32[64,256]{1,0:T(8,128)S(1)} all-gather(f32[16,256]{1,0:T(8,128)S(1)} %convert_reduce_fusion.1), channel_id=2, replica_groups={{0,128,256,384},{32,160,288,416},{64,192,320,448},{96,224,352,480},{1,1..., dimensions={0}, use_global_device_ids=true | all-gather | bytes 81920 | tf_op jit(solution)/shard_map/all_gather | solution.py:165
  53.8 1.8 %all-gather.1 = f32[32,256]{1,0:T(8,128)S(1)} all-gather(f32[16,256]{1,0:T(8,128)S(1)} %reduce_sum.47), channel_id=3, replica_groups={{0,32},{64,96},{128,160},{192,224},{256,288},{320,352},{384,416},{448,4..., dimensions={0}, use_global_device_ids=true | all-gather | bytes 49152 | tf_op jit(solution)/shard_map/all_gather | solution.py:165
  55.6 8.5 %all-gather.2 = f32[32,256]{1,0:T(8,128)S(1)} all-gather(f32[16,256]{1,0:T(8,128)S(1)} %reduce_sum.48), channel_id=4, replica_groups={{0,64},{32,96},{128,192},{160,224},{256,320},{288,352},{384,448},{416,4..., dimensions={0}, use_global_device_ids=true | all-gather | bytes 49152 | tf_op jit(solution)/shard_map/all_gather | solution.py:165
  64.1 0.7 fusion.code_ref
  64.9 3.2 %all-to-all-done = f16[32,64,256]{2,1,0:T(8,128)(2,1)S(1)} async-done(((f16[32,64,256]{2,1,0:T(8,128)(2,1)}), f16[32,64,256]{2,1,0:T(8,128)(2,1)S(1)}, u32[]{:S(2)}, u32[]{:S(2)}) %all-to-all-start) | async-done | bytes 1048608 | tf_op jit(solution)/shard_map/all_to_all | solution.py:260
  68.1 0.2 convert_reduce_fusion.total_ref
  68.2 0.0 copy-start
  68.3 1.4 %spread.1 = bf16[32,80,256]{2,1,0:T(8,128)(2,1)} custom-call(f32[64,256]{1,0:T(8,128)S(1)} %convert_reduce_fusion.total_ref, bf16[64,256]{1,0:T(8,128)(2,1)S(1)} %constant_dynamic-slice_fusion.left_ref, bf16[16,256]{1,0:T(8,128)(2,1)S(1)} %fusion.code_ref), custom_call_target="tpu_custom_call" | custom-call | tf_op jit(solution)/shard_map/spread/pallas_call | solution.py:182
  69.6 6.9 %all-to-all-start.2 = ((bf16[32,80,256]{2,1,0:T(8,128)(2,1)}), bf16[32,80,256]{2,1,0:T(8,128)(2,1)S(1)}, u32[]{:S(2)}, u32[]{:S(2)}) async-start(bf16[32,80,256]{2,1,0:T(8,128)(2,1)} %spread.1), calls=%async_computation.2 | async-start | bytes 2621440 | tf_op jit(solution)/shard_map/all_to_all | solution.py:268
  76.5 0.0 copy-done
  76.5 3.4 %collective-permute-start = (bf16[1,512,256]{2,1,0:T(8,128)(2,1)S(1)}, bf16[1,512,256]{2,1,0:T(8,128)(2,1)S(1)}, u32[]{:S(2)}, u32[]{:S(2)}) collective-permute-start(bf16[1,512,256]{2,1,0:T(8,128)(2,1)S(1)} %bitcast.20), channel_id=1, source_target_pairs={{0,1},{1,2},{2,3},{3,4},{4,5},{5,6},{6,7},{7,8},{8,9},{9,10},{10,1... | collective-permute-start | bytes 786440 | tf_op jit(solution)/shard_map/ppermute | solution.py:20
  79.9 34.5 %collective-permute-done.block_ref = bf16[1,512,256]{2,1,0:T(8,128)(2,1)S(1)} collective-permute-done((bf16[1,512,256]{2,1,0:T(8,128)(2,1)S(1)}, bf16[1,512,256]{2,1,0:T(8,128)(2,1)S(1)}, u32[]{:S(2)}, u32[]{:S(2)}) %collective-permute-start) | collective-permute-done | bytes 262176 | tf_op jit(solution)/shard_map/ppermute | solution.py:20
  114.4 0.7 settle.1
  115.1 0.0 all-to-all-done.2.got_ref
  115.1 1.2 finish.1
  (4 shorter events, 0.1 us)
Async XLA Ops:
  8.9 24.5 %all-to-all-start.1 = ((bf16[32,16,256]{2,1,0:T(8,128)(2,1)}), bf16[32,16,256]{2,1,0:T(8,128)(2,1)S(1)}, u32[]{:S(2)}, u32[]{:S(2)}) async-start(bf16[32,16,256]{2,1,0:T(8,128)(2,1)} %bitcast.13), calls=%async_computation.1 | async-start | bytes 524288 | tf_op jit(solution)/shard_map/all_to_all | solution.py:256
  33.4 34.7 %all-to-all-start = ((f16[32,64,256]{2,1,0:T(8,128)(2,1)}), f16[32,64,256]{2,1,0:T(8,128)(2,1)S(1)}, u32[]{:S(2)}, u32[]{:S(2)}) async-start(f16[32,64,256]{2,1,0:T(8,128)(2,1)} %bitcast.3), calls=%async_computation | async-start | bytes 2097152 | tf_op jit(solution)/shard_map/all_to_all | solution.py:260
  68.2 8.3 %copy-start = (bf16[512,256]{1,0:T(8,128)(2,1)S(1)}, bf16[512,256]{1,0:T(8,128)(2,1)}, u32[]{:S(2)}) copy-start(bf16[512,256]{1,0:T(8,128)(2,1)} %get-tuple-element.13) | copy-start | bytes 786436
  69.6 45.5 %all-to-all-start.2 = ((bf16[32,80,256]{2,1,0:T(8,128)(2,1)}), bf16[32,80,256]{2,1,0:T(8,128)(2,1)S(1)}, u32[]{:S(2)}, u32[]{:S(2)}) async-start(bf16[32,80,256]{2,1,0:T(8,128)(2,1)} %spread.1), calls=%async_computation.2 | async-start | bytes 2621440 | tf_op jit(solution)/shard_map/all_to_all | solution.py:268
  76.5 37.9 %collective-permute-start = (bf16[1,512,256]{2,1,0:T(8,128)(2,1)S(1)}, bf16[1,512,256]{2,1,0:T(8,128)(2,1)S(1)}, u32[]{:S(2)}, u32[]{:S(2)}) collective-permute-start(bf16[1,512,256]{2,1,0:T(8,128)(2,1)S(1)} %bitcast.20), channel_id=1, source_target_pairs={{0,1},{1,2},{2,3},{3,4},{4,5},{5,6},{6,7},{7,8},{8,9},{9,10},{10,1... | collective-permute-start | bytes 786440 | tf_op jit(solution)/shard_map/ppermute | solution.py:20

commit v5 on v4

--- a/solution.py
+++ b/solution.py
@@ -28,51 +28,53 @@
     return lax.dot_general(a, b, (((1,), (1,)), ((), ())), preferred_element_type=F32)
 
 
+def mm_tn(a, b):
+    return lax.dot_general(a, b, (((0,), (0,)), ((), ())), preferred_element_type=F32)
+
+
 def two_parts(x):
     high = x.astype(BF16)
     return high, (x - high.astype(F32)).astype(BF16)
 
 
 def one_hot(rows, ids):
-    return jnp.where(lax.broadcasted_iota(jnp.int32, (rows, ids.shape[1]), 0) == ids, 1.0, 0.0)
+    places = lax.broadcasted_iota(jnp.int32, (rows, ids.shape[1]), 0)
+    return jnp.where(places.astype(jnp.int16) == ids.astype(jnp.int16), BF16(1), BF16(0))
 
 
 def edge_kernel(
     count_ref, src_ref, kind_ref, dst_ref, neg_ref, left_ref, right_ref, rel_ref,
     gh_high_ref, gh_low_ref, rgrad_ref, right_new_ref,
-    left_t, right_t, rel_high_t, rel_low_t, rgrad, tgrad,
+    right_t, rgrad, tgrad,
 ):
     n_left, width = left_ref.shape
     n_right, n_rel = right_ref.shape[0], rel_ref.shape[0]
     half = width // 2
     blocks = src_ref.shape[0]
     negs = neg_ref.shape[0] * neg_ref.shape[2]
-    count = count_ref[0]
+    count = count_ref[...]
     eye = jnp.where(
         lax.broadcasted_iota(jnp.int32, (width, width), 0)
         == lax.broadcasted_iota(jnp.int32, (width, width), 1),
         1.0,
         0.0,
     ).astype(BF16)
-    left_t[...] = mm_nt(eye, left_ref[...]).astype(BF16)
     right_t[...] = mm_nt(eye, right_ref[...]).astype(BF16)
     rel_high, rel_low = two_parts(rel_ref[...])
-    rel_high_t[...] = mm_nt(eye, rel_high).astype(BF16)
-    rel_low_t[...] = mm_nt(eye, rel_low).astype(BF16)
-    seen = one_hot(n_right, neg_ref[0])
+    seen = one_hot(n_right, neg_ref[0]).astype(F32)
     for i in range(1, neg_ref.shape[0]):
-        seen = seen + one_hot(n_right, neg_ref[i])
+        seen = seen + one_hot(n_right, neg_ref[i]).astype(F32)
     times = jnp.sum(seen, axis=1, keepdims=True) * (1.0 / negs)
     rgrad[...] = jnp.zeros_like(rgrad)
     tgrad[...] = jnp.zeros_like(tgrad)
 
     def block(i, carry):
-        ohs = one_hot(n_left, src_ref[i]).astype(BF16)
-        ohk = one_hot(n_rel, kind_ref[i]).astype(BF16)
-        ohd = one_hot(n_right, dst_ref[i]).astype(BF16)
-        head = mm(left_t[...], ohs)
+        ohs = one_hot(n_left, src_ref[i])
+        ohk = one_hot(n_rel, kind_ref[i])
+        ohd = one_hot(n_right, dst_ref[i])
+        head = mm_tn(left_ref[...], ohs)
         tail = mm(right_t[...], ohd)
-        rel = mm(rel_high_t[...], ohk) + mm(rel_low_t[...], ohk)
+        rel = mm_tn(rel_high, ohk) + mm_tn(rel_low, ohk)
         hre, him = head[:half], head[half:]
         rre, rim = rel[:half], rel[half:]
         query = jnp.concatenate([hre * rre - him * rim, hre * rim + him * rre], axis=0)
@@ -106,7 +108,7 @@
         start = pl.multiple_of(j * ROWS, ROWS)
         total = jnp.zeros((ROWS, width), F32)
         for i in range(blocks):
-            hot = one_hot(ROWS, src_ref[i] - start).astype(BF16)
+            hot = one_hot(ROWS, src_ref[i] - start)
             total += mm_nt(hot, gh_high_ref[i]) + mm_nt(hot, gh_low_ref[i])
         lgrad_ref[pl.ds(start, ROWS), :] = total
         return carry
@@ -118,7 +120,7 @@
 
 
 def edge_grads(count, src, kind, dst, neg, left_blk, right_blk, relations, interpret=False):
-    n_left, width = left_blk.shape
+    _, width = left_blk.shape
     n_right, n_rel, blocks = right_blk.shape[0], relations.shape[0], src.shape[0]
     return pl.pallas_call(
         edge_kernel,
@@ -128,13 +130,10 @@
             jax.ShapeDtypeStruct((n_rel, width), BF16),
             jax.ShapeDtypeStruct((n_right, width), BF16),
         ),
-        in_specs=[pl.BlockSpec(memory_space=pltpu.SMEM)] + [VMEM] * 7,
+        in_specs=[VMEM] * 8,
         out_specs=(VMEM,) * 4,
         scratch_shapes=[
-            pltpu.VMEM((width, n_left), BF16),
             pltpu.VMEM((width, n_right), BF16),
-            pltpu.VMEM((width, n_rel), BF16),
-            pltpu.VMEM((width, n_rel), BF16),
             pltpu.VMEM((n_rel, width), F32),
             pltpu.VMEM((n_right, width), F32),
         ],
@@ -250,7 +249,7 @@
         ids.reshape(-1, 1, EDGES) for ids in (source_ids, relation_ids, target_ids, negative_ids)
     )
     gh_high, gh_low, rel_grad, updated = edge_grads(
-        edge_counts.reshape(1), src, kind, dst, neg, left_table, right_table[0], relations
+        edge_counts, src, kind, dst, neg, left_table, right_table[0], relations
     )
     moved = passed_along(updated[None], "right", 1)
     rel_got = lax.all_to_all(rel_grad.reshape(peers, own_rel, width), "right", 0, 0)

time: 117 us -> 116 us (level)
  no operation moved by 1% of the time
where the time goes in v5:
time: 116 us
  waiting for transfers between devices  40.5 us (35%)
  starting transfers between devices  31.4 us (27%)
  blocking collectives  22.5 us (19%)
  Pallas kernels  15.3 us (13%)
  other arithmetic  3.67 us (3%)
  between operations  1.36 us (1%)
    ppermute x1, waiting for transfers between devices, passed_along(): lax.ppermute(array, axis, [(i, (i + by) % peers) for i in range(peers)])  34.5 us
    all_gather x3, blocking collectives, summed_over(): lax.all_gather(part, axis, axis=0, axis_index_groups=groups)  22.5 us
    all_to_all x1, starting transfers between devices, shards(): lax.all_to_all(rel_grad.reshape(peers, own_rel, width), 'right', 0, 0)  13.9 us
    all_to_all x1, starting transfers between devices, shards(): left_got = lax.all_to_all(sent, 'right', 0, 0)  7.34 us
    pallas_call x1, Pallas kernels, edge_grads(): pl.pallas_call(edge_kernel, out_shape=(jax.ShapeDtypeStruct((blocks, widt...  6.94 us
    all_to_all x1, starting transfers between devices, shards(): lax.all_to_all(for_all(left_total, left_rows, code, peers), 'right', 0, 0)  6.88 us
    pallas_call x1, Pallas kernels, left_sums(): pl.pallas_call(left_kernel, out_shape=jax.ShapeDtypeStruct((n_left, width...  5.14 us
    ppermute x1, starting transfers between devices, passed_along(): lax.ppermute(array, axis, [(i, (i + by) % peers) for i in range(peers)])  3.37 us
  transfers between devices with their start and end apart: 4, of which 3 were waited for; matrix products, arithmetic and copies ran while one was open for 4% of the time, Pallas kernels for 5%

profile of v5, /device:TPU:16, one launch (start us, length us, event | category | flops | bytes accessed | tf_op | source)
XLA Modules:
  0.0 115.6 jit_solution(12425249322248065875)
XLA Ops:
  1.3 6.9 %edges.1 = (bf16[1,256,1024]{2,1,0:T(8,128)(2,1)}, bf16[1,256,1024]{2,1,0:T(8,128)(2,1)}, bf16[512,256]{1,0:T(8,128)(2,1)}, bf16[512,256]{1,0:T(8,128)(2,1)}) custom-call(s32[1,1]{1,0:T(1,128)S(6)} %copy.11.count_ref, s32[1,1,1024]{2,1,0:T(1,128)} %src_ref.3, s32[1,1,1024]{2,1,0:T(1,128)} %kind_ref.1, s32[1,1,1024]{2,1,0:T(1,128)} %dst_ref.1, ...), custom_call_target="tpu_custom_call" | custom-call | tf_op jit(solution)/shard_map/edges/pallas_call | solution.py:125
  8.2 13.9 %all-to-all-start.1 = ((bf16[32,16,256]{2,1,0:T(8,128)(2,1)}), bf16[32,16,256]{2,1,0:T(8,128)(2,1)S(1)}, u32[]{:S(2)}, u32[]{:S(2)}) async-start(bf16[32,16,256]{2,1,0:T(8,128)(2,1)} %bitcast.11), calls=%async_computation.1 | async-start | bytes 524288 | tf_op jit(solution)/shard_map/all_to_all | solution.py:255
  22.1 5.1 %leftrows.1 = f32[2048,256]{1,0:T(8,128)} custom-call(s32[1,1,1024]{2,1,0:T(1,128)} %src_ref.3, bf16[1,256,1024]{2,1,0:T(8,128)(2,1)} %get-tuple-element.9.gh_high_ref, bf16[1,256,1024]{2,1,0:T(8,128)(2,1)} %get-tuple-element.10.gh_low_ref), custom_call_target="tpu_custom_call" | custom-call | flops 2147483648 | bytes 4194304 | tf_op jit(solution)/shard_map/leftrows/pallas_call | solution.py:147
  27.2 2.7 %convert_element_type.12 = f16[2048,256]{1,0:T(8,128)(2,1)} convert(f32[2048,256]{1,0:T(8,128)} %leftrows.1) | non-fusion elementwise | flops 524288 | bytes 3145728 | tf_op jit(solution)/shard_map/convert_element_type | solution.py:257
  29.9 2.8 %all-to-all-done.1 = bf16[32,16,256]{2,1,0:T(8,128)(2,1)S(1)} async-done(((bf16[32,16,256]{2,1,0:T(8,128)(2,1)}), bf16[32,16,256]{2,1,0:T(8,128)(2,1)S(1)}, u32[]{:S(2)}, u32[]{:S(2)}) %all-to-all-start.1) | async-done | bytes 262176 | tf_op jit(solution)/shard_map/all_to_all | solution.py:255
  32.7 7.3 %all-to-all-start = ((f16[32,64,256]{2,1,0:T(8,128)(2,1)}), f16[32,64,256]{2,1,0:T(8,128)(2,1)S(1)}, u32[]{:S(2)}, u32[]{:S(2)}) async-start(f16[32,64,256]{2,1,0:T(8,128)(2,1)} %bitcast.2), calls=%async_computation | async-start | bytes 2097152 | tf_op jit(solution)/shard_map/all_to_all | solution.py:259
  40.1 0.8 constant_dynamic-slice_fusion.left_ref
  40.9 12.2 %all-gather = f32[64,256]{1,0:T(8,128)S(1)} all-gather(f32[16,256]{1,0:T(8,128)S(1)} %convert_reduce_fusion.1), channel_id=2, replica_groups={{0,128,256,384},{32,160,288,416},{64,192,320,448},{96,224,352,480},{1,1..., dimensions={0}, use_global_device_ids=true | all-gather | bytes 81920 | tf_op jit(solution)/shard_map/all_gather | solution.py:164
  53.1 1.8 %all-gather.1 = f32[32,256]{1,0:T(8,128)S(1)} all-gather(f32[16,256]{1,0:T(8,128)S(1)} %reduce_sum.47), channel_id=3, replica_groups={{0,32},{64,96},{128,160},{192,224},{256,288},{320,352},{384,416},{448,4..., dimensions={0}, use_global_device_ids=true | all-gather | bytes 49152 | tf_op jit(solution)/shard_map/all_gather | solution.py:164
  55.0 8.5 %all-gather.2 = f32[32,256]{1,0:T(8,128)S(1)} all-gather(f32[16,256]{1,0:T(8,128)S(1)} %reduce_sum.48), channel_id=4, replica_groups={{0,64},{32,96},{128,192},{160,224},{256,320},{288,352},{384,448},{416,4..., dimensions={0}, use_global_device_ids=true | all-gather | bytes 49152 | tf_op jit(solution)/shard_map/all_gather | solution.py:164
  63.5 0.7 fusion.code_ref
  64.2 3.2 %all-to-all-done = f16[32,64,256]{2,1,0:T(8,128)(2,1)S(1)} async-done(((f16[32,64,256]{2,1,0:T(8,128)(2,1)}), f16[32,64,256]{2,1,0:T(8,128)(2,1)S(1)}, u32[]{:S(2)}, u32[]{:S(2)}) %all-to-all-start) | async-done | bytes 1048608 | tf_op jit(solution)/shard_map/all_to_all | solution.py:259
  67.4 0.2 convert_reduce_fusion.total_ref
  67.6 0.0 copy-start
  67.6 1.4 %spread.1 = bf16[32,80,256]{2,1,0:T(8,128)(2,1)} custom-call(f32[64,256]{1,0:T(8,128)S(1)} %convert_reduce_fusion.total_ref, bf16[64,256]{1,0:T(8,128)(2,1)S(1)} %constant_dynamic-slice_fusion.left_ref, bf16[16,256]{1,0:T(8,128)(2,1)S(1)} %fusion.code_ref), custom_call_target="tpu_custom_call" | custom-call | tf_op jit(solution)/shard_map/spread/pallas_call | solution.py:181
  68.9 6.9 %all-to-all-start.2 = ((bf16[32,80,256]{2,1,0:T(8,128)(2,1)}), bf16[32,80,256]{2,1,0:T(8,128)(2,1)S(1)}, u32[]{:S(2)}, u32[]{:S(2)}) async-start(bf16[32,80,256]{2,1,0:T(8,128)(2,1)} %spread.1), calls=%async_computation.2 | async-start | bytes 2621440 | tf_op jit(solution)/shard_map/all_to_all | solution.py:267
  75.8 0.0 copy-done
  75.8 3.4 %collective-permute-start = (bf16[1,512,256]{2,1,0:T(8,128)(2,1)S(1)}, bf16[1,512,256]{2,1,0:T(8,128)(2,1)S(1)}, u32[]{:S(2)}, u32[]{:S(2)}) collective-permute-start(bf16[1,512,256]{2,1,0:T(8,128)(2,1)S(1)} %bitcast.18), channel_id=1, source_target_pairs={{0,1},{1,2},{2,3},{3,4},{4,5},{5,6},{6,7},{7,8},{8,9},{9,10},{10,1... | collective-permute-start | bytes 786440 | tf_op jit(solution)/shard_map/ppermute | solution.py:20
  79.2 34.5 %collective-permute-done.block_ref = bf16[1,512,256]{2,1,0:T(8,128)(2,1)S(1)} collective-permute-done((bf16[1,512,256]{2,1,0:T(8,128)(2,1)S(1)}, bf16[1,512,256]{2,1,0:T(8,128)(2,1)S(1)}, u32[]{:S(2)}, u32[]{:S(2)}) %collective-permute-start) | collective-permute-done | bytes 262176 | tf_op jit(solution)/shard_map/ppermute | solution.py:20
  113.7 0.7 settle.1
  114.4 0.0 all-to-all-done.2.got_ref
  114.4 1.2 %finish.1 = (bf16[32,64,256]{2,1,0:T(8,128)(2,1)}, f32[32,16,256]{2,1,0:T(8,128)}) custom-call(bf16[32,80,256]{2,1,0:T(8,128)(2,1)S(1)} %all-to-all-done.2.got_ref), custom_call_target="tpu_custom_call" | custom-call | tf_op jit(solution)/shard_map/finish/pallas_call | solution.py:226
  (4 shorter events, 0.1 us)
Async XLA Ops:
  8.2 24.5 %all-to-all-start.1 = ((bf16[32,16,256]{2,1,0:T(8,128)(2,1)}), bf16[32,16,256]{2,1,0:T(8,128)(2,1)S(1)}, u32[]{:S(2)}, u32[]{:S(2)}) async-start(bf16[32,16,256]{2,1,0:T(8,128)(2,1)} %bitcast.11), calls=%async_computation.1 | async-start | bytes 524288 | tf_op jit(solution)/shard_map/all_to_all | solution.py:255
  32.7 34.7 %all-to-all-start = ((f16[32,64,256]{2,1,0:T(8,128)(2,1)}), f16[32,64,256]{2,1,0:T(8,128)(2,1)S(1)}, u32[]{:S(2)}, u32[]{:S(2)}) async-start(f16[32,64,256]{2,1,0:T(8,128)(2,1)} %bitcast.2), calls=%async_computation | async-start | bytes 2097152 | tf_op jit(solution)/shard_map/all_to_all | solution.py:259
  67.6 8.3 %copy-start = (bf16[512,256]{1,0:T(8,128)(2,1)S(1)}, bf16[512,256]{1,0:T(8,128)(2,1)}, u32[]{:S(2)}) copy-start(bf16[512,256]{1,0:T(8,128)(2,1)} %get-tuple-element.13) | copy-start | bytes 786436
  68.9 45.5 %all-to-all-start.2 = ((bf16[32,80,256]{2,1,0:T(8,128)(2,1)}), bf16[32,80,256]{2,1,0:T(8,128)(2,1)S(1)}, u32[]{:S(2)}, u32[]{:S(2)}) async-start(bf16[32,80,256]{2,1,0:T(8,128)(2,1)} %spread.1), calls=%async_computation.2 | async-start | bytes 2621440 | tf_op jit(solution)/shard_map/all_to_all | solution.py:267
  75.8 37.9 %collective-permute-start = (bf16[1,512,256]{2,1,0:T(8,128)(2,1)S(1)}, bf16[1,512,256]{2,1,0:T(8,128)(2,1)S(1)}, u32[]{:S(2)}, u32[]{:S(2)}) collective-permute-start(bf16[1,512,256]{2,1,0:T(8,128)(2,1)S(1)} %bitcast.18), channel_id=1, source_target_pairs={{0,1},{1,2},{2,3},{3,4},{4,5},{5,6},{6,7},{7,8},{8,9},{9,10},{10,1... | collective-permute-start | bytes 786440 | tf_op jit(solution)/shard_map/ppermute | solution.py:20

commit v6 on v5

--- a/solution.py
+++ b/solution.py
@@ -44,7 +44,7 @@
 
 def edge_kernel(
     count_ref, src_ref, kind_ref, dst_ref, neg_ref, left_ref, right_ref, rel_ref,
-    gh_high_ref, gh_low_ref, rgrad_ref, right_new_ref,
+    gh_high_ref, gh_low_ref, rgrad_ref, right_new_ref, own_ref,
     right_t, rgrad, tgrad,
 ):
     n_left, width = left_ref.shape
@@ -98,6 +98,8 @@
     lax.fori_loop(0, blocks, block, 0)
     rgrad_ref[...] = rgrad[...].astype(BF16)
     right_new_ref[...] = (right_ref[...].astype(F32) - step_size * tgrad[...]).astype(BF16)
+    own = own_ref.shape[0]
+    own_ref[...] = left_ref[pl.ds(pl.multiple_of(lax.axis_index("right") * own, own), own), :]
 
 
 def left_kernel(src_ref, gh_high_ref, gh_low_ref, lgrad_ref):
@@ -119,7 +121,7 @@
 VMEM = pl.BlockSpec(memory_space=pltpu.VMEM)
 
 
-def edge_grads(count, src, kind, dst, neg, left_blk, right_blk, relations, interpret=False):
+def edge_grads(own_left, count, src, kind, dst, neg, left_blk, right_blk, relations, interpret=False):
     _, width = left_blk.shape
     n_right, n_rel, blocks = right_blk.shape[0], relations.shape[0], src.shape[0]
     return pl.pallas_call(
@@ -129,9 +131,10 @@
             jax.ShapeDtypeStruct((blocks, width, EDGES), BF16),
             jax.ShapeDtypeStruct((n_rel, width), BF16),
             jax.ShapeDtypeStruct((n_right, width), BF16),
+            jax.ShapeDtypeStruct((own_left, width), BF16),
         ),
         in_specs=[VMEM] * 8,
-        out_specs=(VMEM,) * 4,
+        out_specs=(VMEM,) * 5,
         scratch_shapes=[
             pltpu.VMEM((width, n_right), BF16),
             pltpu.VMEM((n_rel, width), F32),
@@ -152,14 +155,15 @@
         cost_estimate=pl.CostEstimate(
             flops=4 * n_left * src.size * width, transcendentals=0, bytes_accessed=8 * n_left * width
         ),
+        compiler_params=pltpu.CompilerParams(vmem_limit_bytes=32 * 2**20),
         interpret=interpret,
         name="leftrows",
-    )(src, gh_high, gh_low)
+    )(*(pltpu.with_memory_space_constraint(a, pltpu.HBM) for a in (src, gh_high, gh_low)))
 
 
 def summed_over(part, axis, sizes):
     peers = np.arange(lax.axis_size(axis)).reshape(sizes)
-    for dim in (0, 2, 1):
+    for dim in (1, 0, 3, 2):
         groups = np.moveaxis(peers, dim, -1).reshape(-1, sizes[dim]).tolist()
         part = jnp.sum(lax.all_gather(part, axis, axis=0, axis_index_groups=groups), axis=0)
     return part
@@ -248,8 +252,8 @@
     src, kind, dst, neg = (
         ids.reshape(-1, 1, EDGES) for ids in (source_ids, relation_ids, target_ids, negative_ids)
     )
-    gh_high, gh_low, rel_grad, updated = edge_grads(
-        edge_counts, src, kind, dst, neg, left_table, right_table[0], relations
+    gh_high, gh_low, rel_grad, updated, left_rows = edge_grads(
+        own_left, edge_counts, src, kind, dst, neg, left_table, right_table[0], relations
     )
     moved = passed_along(updated[None], "right", 1)
     rel_got = lax.all_to_all(rel_grad.reshape(peers, own_rel, width), "right", 0, 0)
@@ -257,10 +261,9 @@
     sent = left_grad.astype(jnp.float16).reshape(peers, own_left, width)
     rel_part = jnp.sum(rel_got.astype(F32), axis=0)
     left_got = lax.all_to_all(sent, "right", 0, 0)
-    rel_total = summed_over(rel_part, "left", (4, 2, 2))
+    rel_total = summed_over(rel_part, "left", (2, 2, 2, 2))
     rel_rows = lax.dynamic_slice_in_dim(relations, mine * own_rel, own_rel, 0)
     rel_rows = rel_rows - relation_step * rel_total
-    left_rows = lax.dynamic_slice_in_dim(left_table, mine * own_left, own_left, 0)
     left_total = jnp.sum(left_got.astype(F32), axis=0)
     squares = rel_rows * rel_rows
     code = (jnp.where(rel_rows < 0, -squares, squares) * squares).astype(BF16)

time: 116 us -> 115 us (level)
  the two profiles are of different devices: /device:TPU:16 before, /device:TPU:22 now
where the time goes in v6:
time: 115 us; the launch traced here: 114 us
  waiting for transfers between devices  46 us (40%)
  starting transfers between devices  29.1 us (25%)
  blocking collectives  21.6 us (19%)
  Pallas kernels  13.9 us (12%)
  other arithmetic  2.09 us (2%)
  between operations  1.38 us (1%)
    ppermute x1, waiting for transfers between devices, passed_along(): lax.ppermute(array, axis, [(i, (i + by) % peers) for i in range(peers)])  34.5 us
    all_gather x4, blocking collectives, summed_over(): lax.all_gather(part, axis, axis=0, axis_index_groups=groups)  21.6 us
    all_to_all x1, starting transfers between devices, shards(): lax.all_to_all(rel_grad.reshape(peers, own_rel, width), 'right', 0, 0)  13.8 us
    pallas_call x1, Pallas kernels, edge_grads(): pl.pallas_call(edge_kernel, out_shape=(jax.ShapeDtypeStruct((blocks, widt...  6.93 us
    all_to_all x1, starting transfers between devices, shards(): lax.all_to_all(for_all(left_total, left_rows, code, peers), 'right', 0, 0)  5.98 us
    all_to_all x1, starting transfers between devices, shards(): left_got = lax.all_to_all(sent, 'right', 0, 0)  5.9 us
    all_to_all x1, waiting for transfers between devices, shards(): left_got = lax.all_to_all(sent, 'right', 0, 0)  5.78 us
    all_to_all x1, waiting for transfers between devices, shards(): lax.all_to_all(rel_grad.reshape(peers, own_rel, width), 'right', 0, 0)  5.72 us
  transfers between devices with their start and end apart: 4, of which 3 were waited for; matrix products, arithmetic and copies ran while one was open for 2% of the time, Pallas kernels for 4%

profile of v6, /device:TPU:22, one launch (start us, length us, event | category | flops | bytes accessed | tf_op | source)
XLA Modules:
  0.0 114.1 jit_solution(56888710551782240)
XLA Ops:
  1.3 6.9 %edges.1 = (bf16[1,256,1024]{2,1,0:T(8,128)(2,1)}, bf16[1,256,1024]{2,1,0:T(8,128)(2,1)}, bf16[512,256]{1,0:T(8,128)(2,1)}, bf16[512,256]{1,0:T(8,128)(2,1)}, bf16[64,256]{1,0:T(8,128)(2,1)}) custom-call(s32[1,1]{1,0:T(1,128)S(6)} %copy.11.count_ref, s32[1,1,1024]{2,1,0:T(1,128)} %src_ref.3, s32[1,1,1024]{2,1,0:T(1,128)} %kind_ref.1, s32[1,1,1024]{2,1,0:T(1,128)} %dst_ref.1, ...), custom_call_target="tpu_custom_call" | custom-call | tf_op jit(solution)/shard_map/edges/pallas_call | solution.py:127
  8.2 13.8 %all-to-all-start.1 = ((bf16[32,16,256]{2,1,0:T(8,128)(2,1)}), bf16[32,16,256]{2,1,0:T(8,128)(2,1)S(1)}, u32[]{:S(2)}, u32[]{:S(2)}) async-start(bf16[32,16,256]{2,1,0:T(8,128)(2,1)} %bitcast.11), calls=%async_computation.1 | async-start | bytes 524288 | tf_op jit(solution)/shard_map/all_to_all | solution.py:259
  22.1 3.8 %leftrows.1 = f32[2048,256]{1,0:T(8,128)S(1)} custom-call(s32[1,1,1024]{2,1,0:T(1,128)} %src_ref.3, bf16[1,256,1024]{2,1,0:T(8,128)(2,1)} %get-tuple-element.10.gh_high_ref, bf16[1,256,1024]{2,1,0:T(8,128)(2,1)} %get-tuple-element.11.gh_low_ref), custom_call_target="tpu_custom_call" | custom-call | flops 2147483648 | bytes 4194304 | tf_op jit(solution)/shard_map/leftrows/pallas_call | solution.py:150
  25.9 1.1 convert_element_type.12
  27.0 0.0 copy-start
  27.0 5.7 %all-to-all-done.1 = bf16[32,16,256]{2,1,0:T(8,128)(2,1)S(1)} async-done(((bf16[32,16,256]{2,1,0:T(8,128)(2,1)}), bf16[32,16,256]{2,1,0:T(8,128)(2,1)S(1)}, u32[]{:S(2)}, u32[]{:S(2)}) %all-to-all-start.1) | async-done | bytes 262176 | tf_op jit(solution)/shard_map/all_to_all | solution.py:259
  32.7 5.9 %all-to-all-start = ((f16[32,64,256]{2,1,0:T(8,128)(2,1)}), f16[32,64,256]{2,1,0:T(8,128)(2,1)S(1)}, u32[]{:S(2)}, u32[]{:S(2)}) async-start(f16[32,64,256]{2,1,0:T(8,128)(2,1)} %bitcast.2), calls=%async_computation | async-start | bytes 2097152 | tf_op jit(solution)/shard_map/all_to_all | solution.py:263
  38.7 4.4 %all-gather = f32[32,256]{1,0:T(8,128)S(1)} all-gather(f32[16,256]{1,0:T(8,128)S(1)} %convert_reduce_fusion.1), channel_id=2, replica_groups={{0,128},{32,160},{64,192},{96,224},{256,384},{288,416},{320,448},{352,4..., dimensions={0}, use_global_device_ids=true | all-gather | bytes 49152 | tf_op jit(solution)/shard_map/all_gather | solution.py:168
  43.1 5.9 %all-gather.1 = f32[32,256]{1,0:T(8,128)S(1)} all-gather(f32[16,256]{1,0:T(8,128)S(1)} %reduce_sum.56), channel_id=3, replica_groups={{0,256},{32,288},{64,320},{96,352},{128,384},{160,416},{192,448},{224,4..., dimensions={0}, use_global_device_ids=true | all-gather | bytes 49152 | tf_op jit(solution)/shard_map/all_gather | solution.py:168
  49.0 1.8 %all-gather.2 = f32[32,256]{1,0:T(8,128)S(1)} all-gather(f32[16,256]{1,0:T(8,128)S(1)} %reduce_sum.57), channel_id=4, replica_groups={{0,32},{64,96},{128,160},{192,224},{256,288},{320,352},{384,416},{448,4..., dimensions={0}, use_global_device_ids=true | all-gather | bytes 49152 | tf_op jit(solution)/shard_map/all_gather | solution.py:168
  50.8 9.4 %all-gather.3 = f32[32,256]{1,0:T(8,128)S(1)} all-gather(f32[16,256]{1,0:T(8,128)S(1)} %reduce_sum.58), channel_id=5, replica_groups={{0,64},{32,96},{128,192},{160,224},{256,320},{288,352},{384,448},{416,4..., dimensions={0}, use_global_device_ids=true | all-gather | bytes 49152 | tf_op jit(solution)/shard_map/all_gather | solution.py:168
  60.3 0.7 fusion.code_ref
  61.0 5.8 %all-to-all-done = f16[32,64,256]{2,1,0:T(8,128)(2,1)S(1)} async-done(((f16[32,64,256]{2,1,0:T(8,128)(2,1)}), f16[32,64,256]{2,1,0:T(8,128)(2,1)S(1)}, u32[]{:S(2)}, u32[]{:S(2)}) %all-to-all-start) | async-done | bytes 1048608 | tf_op jit(solution)/shard_map/all_to_all | solution.py:263
  66.8 0.2 convert_reduce_fusion.total_ref
  67.0 0.0 copy-start.1
  67.0 0.0 copy-done
  67.0 1.4 %spread.1 = bf16[32,80,256]{2,1,0:T(8,128)(2,1)} custom-call(f32[64,256]{1,0:T(8,128)S(1)} %convert_reduce_fusion.total_ref, bf16[64,256]{1,0:T(8,128)(2,1)S(1)} %copy-done, bf16[16,256]{1,0:T(8,128)(2,1)S(1)} %fusion.code_ref), custom_call_target="tpu_custom_call" | custom-call | tf_op jit(solution)/shard_map/spread/pallas_call | solution.py:185
  68.3 6.0 %all-to-all-start.2 = ((bf16[32,80,256]{2,1,0:T(8,128)(2,1)}), bf16[32,80,256]{2,1,0:T(8,128)(2,1)S(1)}, u32[]{:S(2)}, u32[]{:S(2)}) async-start(bf16[32,80,256]{2,1,0:T(8,128)(2,1)} %spread.1), calls=%async_computation.2 | async-start | bytes 2621440 | tf_op jit(solution)/shard_map/all_to_all | solution.py:270
  74.3 0.0 copy-done.1
  74.3 3.4 %collective-permute-start = (bf16[1,512,256]{2,1,0:T(8,128)(2,1)S(1)}, bf16[1,512,256]{2,1,0:T(8,128)(2,1)S(1)}, u32[]{:S(2)}, u32[]{:S(2)}) collective-permute-start(bf16[1,512,256]{2,1,0:T(8,128)(2,1)S(1)} %bitcast.20), channel_id=1, source_target_pairs={{0,1},{1,2},{2,3},{3,4},{4,5},{5,6},{6,7},{7,8},{8,9},{9,10},{10,1... | collective-permute-start | bytes 786440 | tf_op jit(solution)/shard_map/ppermute | solution.py:20
  77.7 34.5 %collective-permute-done.block_ref = bf16[1,512,256]{2,1,0:T(8,128)(2,1)S(1)} collective-permute-done((bf16[1,512,256]{2,1,0:T(8,128)(2,1)S(1)}, bf16[1,512,256]{2,1,0:T(8,128)(2,1)S(1)}, u32[]{:S(2)}, u32[]{:S(2)}) %collective-permute-start) | collective-permute-done | bytes 262176 | tf_op jit(solution)/shard_map/ppermute | solution.py:20
  112.2 0.7 settle.1
  113.0 0.0 all-to-all-done.2.got_ref
  113.0 1.2 %finish.1 = (bf16[32,64,256]{2,1,0:T(8,128)(2,1)}, f32[32,16,256]{2,1,0:T(8,128)}) custom-call(bf16[32,80,256]{2,1,0:T(8,128)(2,1)S(1)} %all-to-all-done.2.got_ref), custom_call_target="tpu_custom_call" | custom-call | tf_op jit(solution)/shard_map/finish/pallas_call | solution.py:230
  (5 shorter events, 0.1 us)
Async XLA Ops:
  8.2 24.5 %all-to-all-start.1 = ((bf16[32,16,256]{2,1,0:T(8,128)(2,1)}), bf16[32,16,256]{2,1,0:T(8,128)(2,1)S(1)}, u32[]{:S(2)}, u32[]{:S(2)}) async-start(bf16[32,16,256]{2,1,0:T(8,128)(2,1)} %bitcast.11), calls=%async_computation.1 | async-start | bytes 524288 | tf_op jit(solution)/shard_map/all_to_all | solution.py:259
  27.0 40.0 %copy-start = (bf16[64,256]{1,0:T(8,128)(2,1)S(1)}, bf16[64,256]{1,0:T(8,128)(2,1)}, u32[]{:S(2)}) copy-start(bf16[64,256]{1,0:T(8,128)(2,1)} %get-tuple-element.12.left_ref) | copy-start | bytes 98308
  32.7 34.1 %all-to-all-start = ((f16[32,64,256]{2,1,0:T(8,128)(2,1)}), f16[32,64,256]{2,1,0:T(8,128)(2,1)S(1)}, u32[]{:S(2)}, u32[]{:S(2)}) async-start(f16[32,64,256]{2,1,0:T(8,128)(2,1)} %bitcast.2), calls=%async_computation | async-start | bytes 2097152 | tf_op jit(solution)/shard_map/all_to_all | solution.py:263
  67.0 7.4 %copy-start.1 = (bf16[512,256]{1,0:T(8,128)(2,1)S(1)}, bf16[512,256]{1,0:T(8,128)(2,1)}, u32[]{:S(2)}) copy-start(bf16[512,256]{1,0:T(8,128)(2,1)} %get-tuple-element.15) | copy-start | bytes 786436
  68.3 44.6 %all-to-all-start.2 = ((bf16[32,80,256]{2,1,0:T(8,128)(2,1)}), bf16[32,80,256]{2,1,0:T(8,128)(2,1)S(1)}, u32[]{:S(2)}, u32[]{:S(2)}) async-start(bf16[32,80,256]{2,1,0:T(8,128)(2,1)} %spread.1), calls=%async_computation.2 | async-start | bytes 2621440 | tf_op jit(solution)/shard_map/all_to_all | solution.py:270
  74.3 37.9 %collective-permute-start = (bf16[1,512,256]{2,1,0:T(8,128)(2,1)S(1)}, bf16[1,512,256]{2,1,0:T(8,128)(2,1)S(1)}, u32[]{:S(2)}, u32[]{:S(2)}) collective-permute-start(bf16[1,512,256]{2,1,0:T(8,128)(2,1)S(1)} %bitcast.20), channel_id=1, source_target_pairs={{0,1},{1,2},{2,3},{3,4},{4,5},{5,6},{6,7},{7,8},{8,9},{9,10},{10,1... | collective-permute-start | bytes 786440 | tf_op jit(solution)/shard_map/ppermute | solution.py:20

commit v7 on v6

--- a/solution.py
+++ b/solution.py
@@ -121,6 +121,10 @@
 VMEM = pl.BlockSpec(memory_space=pltpu.VMEM)
 
 
+def in_hbm(*arrays):
+    return tuple(pltpu.with_memory_space_constraint(a, pltpu.HBM) for a in arrays)
+
+
 def edge_grads(own_left, count, src, kind, dst, neg, left_blk, right_blk, relations, interpret=False):
     _, width = left_blk.shape
     n_right, n_rel, blocks = right_blk.shape[0], relations.shape[0], src.shape[0]
@@ -140,9 +144,10 @@
             pltpu.VMEM((n_rel, width), F32),
             pltpu.VMEM((n_right, width), F32),
         ],
+        compiler_params=pltpu.CompilerParams(vmem_limit_bytes=40 * 2**20),
         interpret=interpret,
         name="edges",
-    )(count, src, kind, dst, neg, left_blk, right_blk, relations)
+    )(count, *in_hbm(src, kind, dst, neg, left_blk, right_blk, relations))
 
 
 def left_sums(src, gh_high, gh_low, n_left, interpret=False):
@@ -158,7 +163,7 @@
         compiler_params=pltpu.CompilerParams(vmem_limit_bytes=32 * 2**20),
         interpret=interpret,
         name="leftrows",
-    )(*(pltpu.with_memory_space_constraint(a, pltpu.HBM) for a in (src, gh_high, gh_low)))
+    )(*in_hbm(src), gh_high, gh_low)
 
 
 def summed_over(part, axis, sizes):

time: 115 us -> 114 us (level)
  Pallas kernels: 13.9 us -> 12.7 us
  transfers between devices with their start and end apart: 4 -> 4, of which waited for: 3 -> 3; matrix products, arithmetic and copies ran while one was open for 2% -> 2% of each run, Pallas kernels for 4% -> 3%
where the time goes in v7:
time: 114 us; the launch traced here: 113 us
  waiting for transfers between devices  46.6 us (41%)
  starting transfers between devices  29.1 us (26%)
  blocking collectives  21.6 us (19%)
  Pallas kernels  12.7 us (11%)
  other arithmetic  2.09 us (2%)
  between operations  1.36 us (1%)
    ppermute x1, waiting for transfers between devices, passed_along(): lax.ppermute(array, axis, [(i, (i + by) % peers) for i in range(peers)])  34.5 us
    all_gather x4, blocking collectives, summed_over(): lax.all_gather(part, axis, axis=0, axis_index_groups=groups)  21.6 us
    all_to_all x1, starting transfers between devices, shards(): lax.all_to_all(rel_grad.reshape(peers, own_rel, width), 'right', 0, 0)  13.9 us
    all_to_all x1, waiting for transfers between devices, shards(): lax.all_to_all(rel_grad.reshape(peers, own_rel, width), 'right', 0, 0)  6.26 us
    pallas_call x1, Pallas kernels, edge_grads(): pl.pallas_call(edge_kernel, out_shape=(jax.ShapeDtypeStruct((blocks, widt...  6.24 us
    all_to_all x1, starting transfers between devices, shards(): lax.all_to_all(for_all(left_total, left_rows, code, peers), 'right', 0, 0)  5.97 us
    all_to_all x1, starting transfers between devices, shards(): left_got = lax.all_to_all(sent, 'right', 0, 0)  5.9 us
    all_to_all x1, waiting for transfers between devices, shards(): left_got = lax.all_to_all(sent, 'right', 0, 0)  5.78 us
  transfers between devices with their start and end apart: 4, of which 3 were waited for; matrix products, arithmetic and copies ran while one was open for 2% of the time, Pallas kernels for 3%

profile of v7, /device:TPU:22, one launch (start us, length us, event | category | flops | bytes accessed | tf_op | source)
XLA Modules:
  0.0 113.4 jit_solution(11660888060171074482)
XLA Ops:
  1.3 6.2 %edges.1 = (bf16[1,256,1024]{2,1,0:T(8,128)(2,1)S(1)}, bf16[1,256,1024]{2,1,0:T(8,128)(2,1)S(1)}, bf16[512,256]{1,0:T(8,128)(2,1)}, bf16[512,256]{1,0:T(8,128)(2,1)S(1)}, bf16[64,256]{1,0:T(8,128)(2,1)S(1)}) custom-call(s32[1,1]{1,0:T(1,128)S(6)} %copy.11.count_ref, s32[1,1,1024]{2,1,0:T(1,128)} %src_ref.3, s32[1,1,1024]{2,1,0:T(1,128)} %kind_ref.1, ...), custom_call_target="tpu_custom_call" | custom-call | tf_op jit(solution)/shard_map/edges/pallas_call | solution.py:131
  7.5 13.9 %all-to-all-start.1 = ((bf16[32,16,256]{2,1,0:T(8,128)(2,1)}), bf16[32,16,256]{2,1,0:T(8,128)(2,1)S(1)}, u32[]{:S(2)}, u32[]{:S(2)}) async-start(bf16[32,16,256]{2,1,0:T(8,128)(2,1)} %bitcast.3), calls=%async_computation.1 | async-start | bytes 524288 | tf_op jit(solution)/shard_map/all_to_all | solution.py:264
  21.4 3.3 %leftrows.1 = f32[2048,256]{1,0:T(8,128)S(1)} custom-call(s32[1,1,1024]{2,1,0:T(1,128)} %src_ref.3, bf16[1,256,1024]{2,1,0:T(8,128)(2,1)S(1)} %get-tuple-element.10.gh_high_ref, bf16[1,256,1024]{2,1,0:T(8,128)(2,1)S(1)} %get-tuple-element.11.gh_low_ref), custom_call_target="tpu_custom_call" | custom-call | flops 2147483648 | bytes 4194304 | tf_op jit(solution)/shard_map/leftrows/pallas_call | solution.py:155
  24.6 1.1 %convert_element_type.12 = f16[2048,256]{1,0:T(8,128)(2,1)} convert(f32[2048,256]{1,0:T(8,128)S(1)} %leftrows.1) | non-fusion elementwise | flops 524288 | bytes 3145728 | tf_op jit(solution)/shard_map/convert_element_type | solution.py:266
  25.8 6.3 %all-to-all-done.1 = bf16[32,16,256]{2,1,0:T(8,128)(2,1)S(1)} async-done(((bf16[32,16,256]{2,1,0:T(8,128)(2,1)}), bf16[32,16,256]{2,1,0:T(8,128)(2,1)S(1)}, u32[]{:S(2)}, u32[]{:S(2)}) %all-to-all-start.1) | async-done | bytes 262176 | tf_op jit(solution)/shard_map/all_to_all | solution.py:264
  32.0 5.9 %all-to-all-start = ((f16[32,64,256]{2,1,0:T(8,128)(2,1)}), f16[32,64,256]{2,1,0:T(8,128)(2,1)S(1)}, u32[]{:S(2)}, u32[]{:S(2)}) async-start(f16[32,64,256]{2,1,0:T(8,128)(2,1)} %bitcast.2), calls=%async_computation | async-start | bytes 2097152 | tf_op jit(solution)/shard_map/all_to_all | solution.py:268
  38.0 4.4 %all-gather = f32[32,256]{1,0:T(8,128)S(1)} all-gather(f32[16,256]{1,0:T(8,128)S(1)} %convert_reduce_fusion.1), channel_id=2, replica_groups={{0,128},{32,160},{64,192},{96,224},{256,384},{288,416},{320,448},{352,4..., dimensions={0}, use_global_device_ids=true | all-gather | bytes 49152 | tf_op jit(solution)/shard_map/all_gather | solution.py:173
  42.4 5.9 %all-gather.1 = f32[32,256]{1,0:T(8,128)S(1)} all-gather(f32[16,256]{1,0:T(8,128)S(1)} %reduce_sum.56), channel_id=3, replica_groups={{0,256},{32,288},{64,320},{96,352},{128,384},{160,416},{192,448},{224,4..., dimensions={0}, use_global_device_ids=true | all-gather | bytes 49152 | tf_op jit(solution)/shard_map/all_gather | solution.py:173
  48.3 1.8 %all-gather.2 = f32[32,256]{1,0:T(8,128)S(1)} all-gather(f32[16,256]{1,0:T(8,128)S(1)} %reduce_sum.57), channel_id=4, replica_groups={{0,32},{64,96},{128,160},{192,224},{256,288},{320,352},{384,416},{448,4..., dimensions={0}, use_global_device_ids=true | all-gather | bytes 49152 | tf_op jit(solution)/shard_map/all_gather | solution.py:173
  50.1 9.4 %all-gather.3 = f32[32,256]{1,0:T(8,128)S(1)} all-gather(f32[16,256]{1,0:T(8,128)S(1)} %reduce_sum.58), channel_id=5, replica_groups={{0,64},{32,96},{128,192},{160,224},{256,320},{288,352},{384,448},{416,4..., dimensions={0}, use_global_device_ids=true | all-gather | bytes 49152 | tf_op jit(solution)/shard_map/all_gather | solution.py:173
  59.6 0.7 fusion.code_ref
  60.3 5.8 %all-to-all-done = f16[32,64,256]{2,1,0:T(8,128)(2,1)S(1)} async-done(((f16[32,64,256]{2,1,0:T(8,128)(2,1)}), f16[32,64,256]{2,1,0:T(8,128)(2,1)S(1)}, u32[]{:S(2)}, u32[]{:S(2)}) %all-to-all-start) | async-done | bytes 1048608 | tf_op jit(solution)/shard_map/all_to_all | solution.py:268
  66.1 0.2 convert_reduce_fusion.total_ref
  66.3 1.4 %spread.1 = bf16[32,80,256]{2,1,0:T(8,128)(2,1)} custom-call(f32[64,256]{1,0:T(8,128)S(1)} %convert_reduce_fusion.total_ref, bf16[64,256]{1,0:T(8,128)(2,1)S(1)} %get-tuple-element.12.left_ref, bf16[16,256]{1,0:T(8,128)(2,1)S(1)} %fusion.code_ref), custom_call_target="tpu_custom_call" | custom-call | tf_op jit(solution)/shard_map/spread/pallas_call | solution.py:190
  67.6 6.0 %all-to-all-start.2 = ((bf16[32,80,256]{2,1,0:T(8,128)(2,1)}), bf16[32,80,256]{2,1,0:T(8,128)(2,1)S(1)}, u32[]{:S(2)}, u32[]{:S(2)}) async-start(bf16[32,80,256]{2,1,0:T(8,128)(2,1)} %spread.1), calls=%async_computation.2 | async-start | bytes 2621440 | tf_op jit(solution)/shard_map/all_to_all | solution.py:275
  73.6 3.4 %collective-permute-start = (bf16[1,512,256]{2,1,0:T(8,128)(2,1)S(1)}, bf16[1,512,256]{2,1,0:T(8,128)(2,1)S(1)}, u32[]{:S(2)}, u32[]{:S(2)}) collective-permute-start(bf16[1,512,256]{2,1,0:T(8,128)(2,1)S(1)} %bitcast.11), channel_id=1, source_target_pairs={{0,1},{1,2},{2,3},{3,4},{4,5},{5,6},{6,7},{7,8},{8,9},{9,10},{10,1... | collective-permute-start | bytes 786440 | tf_op jit(solution)/shard_map/ppermute | solution.py:20
  77.0 34.5 %collective-permute-done.block_ref = bf16[1,512,256]{2,1,0:T(8,128)(2,1)S(1)} collective-permute-done((bf16[1,512,256]{2,1,0:T(8,128)(2,1)S(1)}, bf16[1,512,256]{2,1,0:T(8,128)(2,1)S(1)}, u32[]{:S(2)}, u32[]{:S(2)}) %collective-permute-start) | collective-permute-done | bytes 262176 | tf_op jit(solution)/shard_map/ppermute | solution.py:20
  111.5 0.7 settle.1
  112.2 0.0 all-to-all-done.2.got_ref
  112.3 1.2 %finish.1 = (bf16[32,64,256]{2,1,0:T(8,128)(2,1)}, f32[32,16,256]{2,1,0:T(8,128)}) custom-call(bf16[32,80,256]{2,1,0:T(8,128)(2,1)S(1)} %all-to-all-done.2.got_ref), custom_call_target="tpu_custom_call" | custom-call | tf_op jit(solution)/shard_map/finish/pallas_call | solution.py:235
  (5 shorter events, 0.1 us)
Async XLA Ops:
  7.5 24.5 %all-to-all-start.1 = ((bf16[32,16,256]{2,1,0:T(8,128)(2,1)}), bf16[32,16,256]{2,1,0:T(8,128)(2,1)S(1)}, u32[]{:S(2)}, u32[]{:S(2)}) async-start(bf16[32,16,256]{2,1,0:T(8,128)(2,1)} %bitcast.3), calls=%async_computation.1 | async-start | bytes 524288 | tf_op jit(solution)/shard_map/all_to_all | solution.py:264
  32.0 34.1 %all-to-all-start = ((f16[32,64,256]{2,1,0:T(8,128)(2,1)}), f16[32,64,256]{2,1,0:T(8,128)(2,1)S(1)}, u32[]{:S(2)}, u32[]{:S(2)}) async-start(f16[32,64,256]{2,1,0:T(8,128)(2,1)} %bitcast.2), calls=%async_computation | async-start | bytes 2097152 | tf_op jit(solution)/shard_map/all_to_all | solution.py:268
  67.6 44.6 %all-to-all-start.2 = ((bf16[32,80,256]{2,1,0:T(8,128)(2,1)}), bf16[32,80,256]{2,1,0:T(8,128)(2,1)S(1)}, u32[]{:S(2)}, u32[]{:S(2)}) async-start(bf16[32,80,256]{2,1,0:T(8,128)(2,1)} %spread.1), calls=%async_computation.2 | async-start | bytes 2621440 | tf_op jit(solution)/shard_map/all_to_all | solution.py:275
  73.6 37.9 %collective-permute-start = (bf16[1,512,256]{2,1,0:T(8,128)(2,1)S(1)}, bf16[1,512,256]{2,1,0:T(8,128)(2,1)S(1)}, u32[]{:S(2)}, u32[]{:S(2)}) collective-permute-start(bf16[1,512,256]{2,1,0:T(8,128)(2,1)S(1)} %bitcast.11), channel_id=1, source_target_pairs={{0,1},{1,2},{2,3},{3,4},{4,5},{5,6},{6,7},{7,8},{8,9},{9,10},{10,1... | collective-permute-start | bytes 786440 | tf_op jit(solution)/shard_map/ppermute | solution.py:20

commit v8 on v7

--- a/solution.py
+++ b/solution.py
@@ -10,7 +10,7 @@
 step_size = 0.5
 relation_step = 12.0
 EDGES = 1024
-ROWS = 1024
+ROWS = 2048
 F32 = jnp.float32
 BF16 = jnp.bfloat16
 
@@ -50,7 +50,6 @@
     n_left, width = left_ref.shape
     n_right, n_rel = right_ref.shape[0], rel_ref.shape[0]
     half = width // 2
-    blocks = src_ref.shape[0]
     negs = neg_ref.shape[0] * neg_ref.shape[2]
     count = count_ref[...]
     eye = jnp.where(
@@ -65,8 +64,6 @@
     for i in range(1, neg_ref.shape[0]):
         seen = seen + one_hot(n_right, neg_ref[i]).astype(F32)
     times = jnp.sum(seen, axis=1, keepdims=True) * (1.0 / negs)
-    rgrad[...] = jnp.zeros_like(rgrad)
-    tgrad[...] = jnp.zeros_like(tgrad)
 
     def block(i, carry):
         ohs = one_hot(n_left, src_ref[i])
@@ -90,14 +87,13 @@
         grad_h = jnp.concatenate([gre * rre + gim * rim, -gre * rim + gim * rre], axis=0)
         grad_r = jnp.concatenate([gre * hre + gim * him, -gre * him + gim * hre], axis=0)
         gh_high_ref[i], gh_low_ref[i] = two_parts(grad_h)
-        rgrad[...] += mm_nt(ohk, grad_r.astype(BF16))
+        rgrad_ref[...] = mm_nt(ohk, grad_r.astype(BF16)).astype(BF16)
         t_high, t_low = two_parts(c_pos * query)
-        tgrad[...] += mm_nt(c_neg, q_low) + mm_nt(ohd, t_high) + mm_nt(ohd, t_low)
+        grad = mm_nt(c_neg, q_low) + mm_nt(ohd, t_high) + mm_nt(ohd, t_low)
+        right_new_ref[...] = (right_ref[...].astype(F32) - step_size * grad).astype(BF16)
         return carry
 
-    lax.fori_loop(0, blocks, block, 0)
-    rgrad_ref[...] = rgrad[...].astype(BF16)
-    right_new_ref[...] = (right_ref[...].astype(F32) - step_size * tgrad[...]).astype(BF16)
+    block(0, 0)
     own = own_ref.shape[0]
     own_ref[...] = left_ref[pl.ds(pl.multiple_of(lax.axis_index("right") * own, own), own), :]
 

time: 114 us -> 114 us (level)
  no operation moved by 1% of the time
where the time goes in v8:
time: 114 us; the launch traced here: 113 us
  waiting for transfers between devices  46.8 us (41%)
  starting transfers between devices  29.1 us (26%)
  blocking collectives  21.6 us (19%)
  Pallas kernels  12.5 us (11%)
  other arithmetic  2.09 us (2%)
  between operations  1.36 us (1%)
    ppermute x1, waiting for transfers between devices, passed_along(): lax.ppermute(array, axis, [(i, (i + by) % peers) for i in range(peers)])  34.5 us
    all_gather x4, blocking collectives, summed_over(): lax.all_gather(part, axis, axis=0, axis_index_groups=groups)  21.6 us
    all_to_all x1, starting transfers between devices, shards(): lax.all_to_all(rel_grad.reshape(peers, own_rel, width), 'right', 0, 0)  13.9 us
    all_to_all x1, waiting for transfers between devices, shards(): lax.all_to_all(rel_grad.reshape(peers, own_rel, width), 'right', 0, 0)  6.44 us
    pallas_call x1, Pallas kernels, edge_grads(): pl.pallas_call(edge_kernel, out_shape=(jax.ShapeDtypeStruct((blocks, widt...  6.24 us
    all_to_all x1, starting transfers between devices, shards(): lax.all_to_all(for_all(left_total, left_rows, code, peers), 'right', 0, 0)  5.97 us
    all_to_all x1, starting transfers between devices, shards(): left_got = lax.all_to_all(sent, 'right', 0, 0)  5.9 us
    all_to_all x1, waiting for transfers between devices, shards(): left_got = lax.all_to_all(sent, 'right', 0, 0)  5.78 us
  transfers between devices with their start and end apart: 4, of which 3 were waited for; matrix products, arithmetic and copies ran while one was open for 2% of the time, Pallas kernels for 3%

profile of v8, /device:TPU:22, one launch (start us, length us, event | category | flops | bytes accessed | tf_op | source)
XLA Modules:
  0.0 113.4 jit_solution(9009400132971786772)
XLA Ops:
  1.3 6.2 %edges.1 = (bf16[1,256,1024]{2,1,0:T(8,128)(2,1)S(1)}, bf16[1,256,1024]{2,1,0:T(8,128)(2,1)S(1)}, bf16[512,256]{1,0:T(8,128)(2,1)}, bf16[512,256]{1,0:T(8,128)(2,1)S(1)}, bf16[64,256]{1,0:T(8,128)(2,1)S(1)}) custom-call(s32[1,1]{1,0:T(1,128)S(6)} %copy.11.count_ref, s32[1,1,1024]{2,1,0:T(1,128)} %src_ref.3, s32[1,1,1024]{2,1,0:T(1,128)} %kind_ref.1, ...), custom_call_target="tpu_custom_call" | custom-call | tf_op jit(solution)/shard_map/edges/pallas_call | solution.py:127
  7.5 13.9 %all-to-all-start.1 = ((bf16[32,16,256]{2,1,0:T(8,128)(2,1)}), bf16[32,16,256]{2,1,0:T(8,128)(2,1)S(1)}, u32[]{:S(2)}, u32[]{:S(2)}) async-start(bf16[32,16,256]{2,1,0:T(8,128)(2,1)} %bitcast.3), calls=%async_computation.1 | async-start | bytes 524288 | tf_op jit(solution)/shard_map/all_to_all | solution.py:260
  21.4 3.1 %leftrows.1 = f32[2048,256]{1,0:T(8,128)S(1)} custom-call(s32[1,1,1024]{2,1,0:T(1,128)} %src_ref.3, bf16[1,256,1024]{2,1,0:T(8,128)(2,1)S(1)} %get-tuple-element.10.gh_high_ref, bf16[1,256,1024]{2,1,0:T(8,128)(2,1)S(1)} %get-tuple-element.11.gh_low_ref), custom_call_target="tpu_custom_call" | custom-call | flops 2147483648 | bytes 4194304 | tf_op jit(solution)/shard_map/leftrows/pallas_call | solution.py:151
  24.5 1.1 %convert_element_type.12 = f16[2048,256]{1,0:T(8,128)(2,1)} convert(f32[2048,256]{1,0:T(8,128)S(1)} %leftrows.1) | non-fusion elementwise | flops 524288 | bytes 3145728 | tf_op jit(solution)/shard_map/convert_element_type | solution.py:262
  25.6 6.4 %all-to-all-done.1 = bf16[32,16,256]{2,1,0:T(8,128)(2,1)S(1)} async-done(((bf16[32,16,256]{2,1,0:T(8,128)(2,1)}), bf16[32,16,256]{2,1,0:T(8,128)(2,1)S(1)}, u32[]{:S(2)}, u32[]{:S(2)}) %all-to-all-start.1) | async-done | bytes 262176 | tf_op jit(solution)/shard_map/all_to_all | solution.py:260
  32.0 5.9 %all-to-all-start = ((f16[32,64,256]{2,1,0:T(8,128)(2,1)}), f16[32,64,256]{2,1,0:T(8,128)(2,1)S(1)}, u32[]{:S(2)}, u32[]{:S(2)}) async-start(f16[32,64,256]{2,1,0:T(8,128)(2,1)} %bitcast.2), calls=%async_computation | async-start | bytes 2097152 | tf_op jit(solution)/shard_map/all_to_all | solution.py:264
  38.0 4.4 %all-gather = f32[32,256]{1,0:T(8,128)S(1)} all-gather(f32[16,256]{1,0:T(8,128)S(1)} %convert_reduce_fusion.1), channel_id=2, replica_groups={{0,128},{32,160},{64,192},{96,224},{256,384},{288,416},{320,448},{352,4..., dimensions={0}, use_global_device_ids=true | all-gather | bytes 49152 | tf_op jit(solution)/shard_map/all_gather | solution.py:169
  42.4 5.9 %all-gather.1 = f32[32,256]{1,0:T(8,128)S(1)} all-gather(f32[16,256]{1,0:T(8,128)S(1)} %reduce_sum.56), channel_id=3, replica_groups={{0,256},{32,288},{64,320},{96,352},{128,384},{160,416},{192,448},{224,4..., dimensions={0}, use_global_device_ids=true | all-gather | bytes 49152 | tf_op jit(solution)/shard_map/all_gather | solution.py:169
  48.3 1.8 %all-gather.2 = f32[32,256]{1,0:T(8,128)S(1)} all-gather(f32[16,256]{1,0:T(8,128)S(1)} %reduce_sum.57), channel_id=4, replica_groups={{0,32},{64,96},{128,160},{192,224},{256,288},{320,352},{384,416},{448,4..., dimensions={0}, use_global_device_ids=true | all-gather | bytes 49152 | tf_op jit(solution)/shard_map/all_gather | solution.py:169
  50.1 9.4 %all-gather.3 = f32[32,256]{1,0:T(8,128)S(1)} all-gather(f32[16,256]{1,0:T(8,128)S(1)} %reduce_sum.58), channel_id=5, replica_groups={{0,64},{32,96},{128,192},{160,224},{256,320},{288,352},{384,448},{416,4..., dimensions={0}, use_global_device_ids=true | all-gather | bytes 49152 | tf_op jit(solution)/shard_map/all_gather | solution.py:169
  59.6 0.7 fusion.code_ref
  60.3 5.8 %all-to-all-done = f16[32,64,256]{2,1,0:T(8,128)(2,1)S(1)} async-done(((f16[32,64,256]{2,1,0:T(8,128)(2,1)}), f16[32,64,256]{2,1,0:T(8,128)(2,1)S(1)}, u32[]{:S(2)}, u32[]{:S(2)}) %all-to-all-start) | async-done | bytes 1048608 | tf_op jit(solution)/shard_map/all_to_all | solution.py:264
  66.1 0.2 convert_reduce_fusion.total_ref
  66.3 1.4 %spread.1 = bf16[32,80,256]{2,1,0:T(8,128)(2,1)} custom-call(f32[64,256]{1,0:T(8,128)S(1)} %convert_reduce_fusion.total_ref, bf16[64,256]{1,0:T(8,128)(2,1)S(1)} %get-tuple-element.12.left_ref, bf16[16,256]{1,0:T(8,128)(2,1)S(1)} %fusion.code_ref), custom_call_target="tpu_custom_call" | custom-call | tf_op jit(solution)/shard_map/spread/pallas_call | solution.py:186
  67.6 6.0 %all-to-all-start.2 = ((bf16[32,80,256]{2,1,0:T(8,128)(2,1)}), bf16[32,80,256]{2,1,0:T(8,128)(2,1)S(1)}, u32[]{:S(2)}, u32[]{:S(2)}) async-start(bf16[32,80,256]{2,1,0:T(8,128)(2,1)} %spread.1), calls=%async_computation.2 | async-start | bytes 2621440 | tf_op jit(solution)/shard_map/all_to_all | solution.py:271
  73.6 3.4 %collective-permute-start = (bf16[1,512,256]{2,1,0:T(8,128)(2,1)S(1)}, bf16[1,512,256]{2,1,0:T(8,128)(2,1)S(1)}, u32[]{:S(2)}, u32[]{:S(2)}) collective-permute-start(bf16[1,512,256]{2,1,0:T(8,128)(2,1)S(1)} %bitcast.11), channel_id=1, source_target_pairs={{0,1},{1,2},{2,3},{3,4},{4,5},{5,6},{6,7},{7,8},{8,9},{9,10},{10,1... | collective-permute-start | bytes 786440 | tf_op jit(solution)/shard_map/ppermute | solution.py:20
  77.0 34.5 %collective-permute-done.block_ref = bf16[1,512,256]{2,1,0:T(8,128)(2,1)S(1)} collective-permute-done((bf16[1,512,256]{2,1,0:T(8,128)(2,1)S(1)}, bf16[1,512,256]{2,1,0:T(8,128)(2,1)S(1)}, u32[]{:S(2)}, u32[]{:S(2)}) %collective-permute-start) | collective-permute-done | bytes 262176 | tf_op jit(solution)/shard_map/ppermute | solution.py:20
  111.5 0.7 settle.1
  112.2 0.0 all-to-all-done.2.got_ref
  112.3 1.2 %finish.1 = (bf16[32,64,256]{2,1,0:T(8,128)(2,1)}, f32[32,16,256]{2,1,0:T(8,128)}) custom-call(bf16[32,80,256]{2,1,0:T(8,128)(2,1)S(1)} %all-to-all-done.2.got_ref), custom_call_target="tpu_custom_call" | custom-call | tf_op jit(solution)/shard_map/finish/pallas_call | solution.py:231
  (5 shorter events, 0.1 us)
Async XLA Ops:
  7.5 24.5 %all-to-all-start.1 = ((bf16[32,16,256]{2,1,0:T(8,128)(2,1)}), bf16[32,16,256]{2,1,0:T(8,128)(2,1)S(1)}, u32[]{:S(2)}, u32[]{:S(2)}) async-start(bf16[32,16,256]{2,1,0:T(8,128)(2,1)} %bitcast.3), calls=%async_computation.1 | async-start | bytes 524288 | tf_op jit(solution)/shard_map/all_to_all | solution.py:260
  32.0 34.1 %all-to-all-start = ((f16[32,64,256]{2,1,0:T(8,128)(2,1)}), f16[32,64,256]{2,1,0:T(8,128)(2,1)S(1)}, u32[]{:S(2)}, u32[]{:S(2)}) async-start(f16[32,64,256]{2,1,0:T(8,128)(2,1)} %bitcast.2), calls=%async_computation | async-start | bytes 2097152 | tf_op jit(solution)/shard_map/all_to_all | solution.py:264
  67.6 44.6 %all-to-all-start.2 = ((bf16[32,80,256]{2,1,0:T(8,128)(2,1)}), bf16[32,80,256]{2,1,0:T(8,128)(2,1)S(1)}, u32[]{:S(2)}, u32[]{:S(2)}) async-start(bf16[32,80,256]{2,1,0:T(8,128)(2,1)} %spread.1), calls=%async_computation.2 | async-start | bytes 2621440 | tf_op jit(solution)/shard_map/all_to_all | solution.py:271
  73.6 37.9 %collective-permute-start = (bf16[1,512,256]{2,1,0:T(8,128)(2,1)S(1)}, bf16[1,512,256]{2,1,0:T(8,128)(2,1)S(1)}, u32[]{:S(2)}, u32[]{:S(2)}) collective-permute-start(bf16[1,512,256]{2,1,0:T(8,128)(2,1)S(1)} %bitcast.11), channel_id=1, source_target_pairs={{0,1},{1,2},{2,3},{3,4},{4,5},{5,6},{6,7},{7,8},{8,9},{9,10},{10,1... | collective-permute-start | bytes 786440 | tf_op jit(solution)/shard_map/ppermute | solution.py:20
